TPU v7x, 512 devices: a whole 4x4x16 slice. The times are simulated.
512 devices in a mesh: seq: 16 (over y, x), table: 32 (over z, core).
Axes of the slice: x: 4, y: 4, z: 16, core: 2. Of those that a mesh axis runs over, the one named last changes fastest.
Arguments:
- events_x: bfloat16 [32, 2048, 512], P('table', 'seq'), may hold values from -6 to 6
- proj: bfloat16 [512, 1536], replicated, may hold values from -0.25 to 0.25
- out_grad: bfloat16 [32, 2048, 512], P('table', 'seq'), may hold values from -6 to 6
- block_mask: int32 [16, 16], replicated, may hold values 0 or 1
- item_ids: int32 [32, 2048], P('table', 'seq'), may hold values from 0 to 16383, as said below
- owner_of: int32 [16384], replicated, may hold values from 0 to 31, as said below
- local_of: int32 [16384], replicated, may hold values from 0 to 511, as said below
- table: bfloat16 [16384, 512], P('table'), may hold values from -3 to 3
- moment: float32 [16384, 512], P('table'), may hold values from -2 to 2
- second: float32 [16384], P('table'), may hold values from 0.05 to 2
Outputs:
- new_table: bfloat16 [16384, 512], P('table')
- new_moment: float32 [16384, 512], P('table')
- new_second: float32 [16384], P('table')
- event_rows: bfloat16 [32, 2048, 512], P('table', 'seq')
Inputs may be any that keep to these rules, and one draw needn't show every extreme that they name: `item_ids`: among the 128 events of one device (one history, one seq index), at most 8 have items of one owner (owner_of); in every draw, for each seq index, some owner gets exactly 8 from the device of every history. owner_of[r] * 512 + local_of[r] takes every value of 0 to 16383 once over the items r. `local_of`: see owner_of.
All inputs are finite; a program needn't handle non-finite values.
Results may differ from a plain program's by a relative error of at most 0.0075.
Values may be sent and summed in bfloat16 or wider, within the bound.
No kernel may reach another device: no remote copies, remote signals or barrier semaphores. Data moves between devices by JAX's collectives and lax.ppermute only.
A program may use at most 64 MiB of HBM per device.

v0:
```python
import math

import jax
import jax.numpy as jnp
from jax import lax
from jax.sharding import PartitionSpec as P

HEADS = 8


first_decay = 0.9
second_decay = 0.99
step_rate = 0.05
epsilon = 1e-08


def block_length(piece_rows):
    block_rows = piece_rows
    while block_rows > 1024 and block_rows % 2 == 0:
        block_rows = block_rows // 2
    return block_rows


def adam_update(item_grad, moment, second, table):
    new_moment = first_decay * moment + (1.0 - first_decay) * item_grad
    new_second = second_decay * second + (1.0 - second_decay) * jnp.mean(
        item_grad * item_grad, axis=1
    )
    new_table = (
        table.astype(jnp.float32)
        - step_rate * new_moment / (jnp.sqrt(new_second) + epsilon)[:, None]
    ).astype(jnp.bfloat16)
    return (new_table, new_moment, new_second)


def body(events_x, proj, out_grad, block_mask, item_ids, owner_of, local_of, table, moment, second):
    tokens = events_x.shape[1]
    features = events_x.shape[2]
    head_size = features // HEADS
    seq_count = lax.axis_size("seq")
    owner_count = lax.axis_size("table")
    position = lax.axis_index("seq")
    history_scale = 1.0 / math.sqrt(tokens * seq_count)
    temper = 1.0 / math.sqrt(head_size)
    block_ids = jnp.arange(seq_count)
    inputs = events_x[0]
    cotangent = out_grad[0]
    projected = jnp.dot(inputs, proj, preferred_element_type=jnp.float32).astype(jnp.bfloat16)
    queries = projected[:, :features]
    key_mat = projected[:, features : 2 * features]
    value_mat = projected[:, 2 * features :]
    own_pos = position * tokens + jnp.arange(tokens)
    visible_col = lax.dynamic_slice_in_dim(block_mask, position, 1, 1)[:, 0]

    def split_heads(matrix):
        return matrix.reshape(matrix.shape[0], HEADS, head_size)

    def pair_terms(query_block, grad_block, key_block, value_block, allowed):
        scores = (
            jnp.einsum(
                "qhe,khe->hqk",
                split_heads(query_block),
                split_heads(key_block),
                preferred_element_type=jnp.float32,
            )
            * temper
        )
        gates = jax.nn.sigmoid(scores)
        weights = (scores * gates * history_scale * allowed).astype(jnp.bfloat16)
        slopes = gates * (1.0 + scores * (1.0 - gates))
        attn_grad = jnp.einsum(
            "qhe,khe->hqk",
            split_heads(grad_block),
            split_heads(value_block),
            preferred_element_type=jnp.float32,
        )
        score_grad = (attn_grad * slopes * (history_scale * temper) * allowed).astype(jnp.bfloat16)
        return (weights, score_grad)

    zero_rows = jnp.zeros((tokens, features), jnp.float32)
    zero_terms = jnp.zeros((tokens * seq_count, features), jnp.float32)
    query_piece = lax.all_gather(queries, "seq", axis=0, tiled=True)
    grad_piece = lax.all_gather(cotangent, "seq", axis=0, tiled=True)
    block_rows = block_length(query_piece.shape[0])

    def advance(block_index, running):
        first_row = block_index * block_rows
        query_block = lax.dynamic_slice_in_dim(query_piece, first_row, block_rows, 0)
        grad_block = lax.dynamic_slice_in_dim(grad_piece, first_row, block_rows, 0)
        query_pos = first_row + jnp.arange(block_rows)
        query_blk = query_pos // tokens
        visible = jnp.any(
            (query_blk[:, None] == block_ids[None, :]) & (visible_col[None, :] == 1), axis=1
        ) | (query_blk == position)
        allowed = (visible[:, None] & (own_pos[None, :] <= query_pos[:, None])).astype(jnp.float32)

        def accumulate(current):
            weights, score_grad = pair_terms(query_block, grad_block, key_mat, value_mat, allowed)
            value_total = current[1] + jnp.einsum(
                "hqk,qhe->khe", weights, split_heads(grad_block), preferred_element_type=jnp.float32
            ).reshape(tokens, features)
            key_total = current[0] + jnp.einsum(
                "hqk,qhe->khe",
                score_grad,
                split_heads(query_block),
                preferred_element_type=jnp.float32,
            ).reshape(tokens, features)
            query_part = jnp.einsum(
                "hqk,khe->qhe", score_grad, split_heads(key_mat), preferred_element_type=jnp.float32
            ).reshape(block_rows, features)
            query_terms = lax.dynamic_update_slice(
                current[2], query_part, (first_row, jnp.int32(0))
            )
            return (key_total, value_total, query_terms)

        return lax.cond(jnp.any(allowed > 0), accumulate, lambda current: current, running)

    key_grad, value_grad, query_terms = lax.fori_loop(
        0, query_piece.shape[0] // block_rows, advance, (zero_rows, zero_rows, zero_terms)
    )
    query_grad = lax.psum_scatter(query_terms, "seq", scatter_dimension=0, tiled=True)
    stacked = jnp.concatenate([query_grad, key_grad, value_grad], axis=1).astype(jnp.bfloat16)
    input_grad = lax.dot_general(
        stacked, proj, (((1,), (1,)), ((), ())), preferred_element_type=jnp.float32
    ).astype(jnp.bfloat16)
    event_items = item_ids[0]
    owners = owner_of[event_items]
    slab_index = local_of[event_items]
    capacity = 2 * tokens // owner_count
    owner_hits = (owners[:, None] == jnp.arange(owner_count)[None, :]).astype(jnp.int32)
    slots = jnp.sum(jnp.cumsum(owner_hits, axis=0) * owner_hits, axis=1) - 1
    target = owners * capacity + slots
    send_rows = (
        jnp.zeros((owner_count * capacity, features), jnp.bfloat16)
        .at[target]
        .set(input_grad)
        .reshape(owner_count, capacity, features)
    )
    send_index = (
        jnp.full((owner_count * capacity,), -1, jnp.int32)
        .at[target]
        .set(slab_index)
        .reshape(owner_count, capacity)
    )
    got_rows, got_index = (
        lax.all_to_all(send_rows, "table", split_axis=0, concat_axis=0, tiled=True),
        lax.all_to_all(send_index, "table", split_axis=0, concat_axis=0, tiled=True),
    )
    slab_rows = table.shape[0]
    select = (got_index.reshape(-1)[None, :] == jnp.arange(slab_rows)[:, None]).astype(jnp.bfloat16)
    slab_grad = jnp.dot(select, got_rows.reshape(-1, features), preferred_element_type=jnp.float32)
    item_grad = lax.psum(slab_grad.astype(jnp.bfloat16), "seq").astype(jnp.float32)
    new_table, new_moment, new_second = adam_update(item_grad, moment, second, table)
    clamped = jnp.clip(got_index, 0, slab_rows - 1)
    replies = jnp.where(
        (got_index >= 0)[:, :, None], new_table[clamped], jnp.zeros((), jnp.bfloat16)
    )
    returned_rows = lax.all_to_all(replies, "table", split_axis=0, concat_axis=0, tiled=True)
    event_rows = returned_rows.reshape(owner_count * capacity, features)[target]
    return (new_table, new_moment, new_second, event_rows[None])


def solution(mesh):
    return jax.shard_map(
        body,
        mesh=mesh,
        in_specs=(
            P("table", "seq", None),
            P(),
            P("table", "seq", None),
            P(),
            P("table", "seq"),
            P(),
            P(),
            P("table", None),
            P("table", None),
            P("table"),
        ),
        out_specs=(P("table", None), P("table", None), P("table"), P("table", "seq", None)),
        check_vma=False,
    )
```

profile of v0, /device:TPU:1, one launch (start us, length us, event | category | flops | bytes accessed | tf_op | source)
XLA Modules:
  0.0 459.3 jit_solution(3907325187602014289)
XLA Ops:
  10.6 1.7 copy.42
  13.5 62.1 %all-gather.4.cloned.1.call-done = bf16[2048,512]{1,0:T(8,128)(2,1)} async-done(((bf16[128,512]{1,0:T(8,128)(2,1)}), bf16[2048,512]{1,0:T(8,128)(2,1)}) %all-gather.4.cloned.1.call-update) | async-done | bytes 2097168 | tf_op jit(solution)/shard_map/all_gather | solution.py:82
  75.5 4.0 copy.44
  79.5 61.6 %all-gather.6.cloned.1.call-done = bf16[1,2048,512]{1,2,0:T(8,128)(2,1)} async-done(((bf16[1,128,512]{1,2,0:T(8,128)(2,1)}), bf16[1,2048,512]{1,2,0:T(8,128)(2,1)}) %all-gather.6.cloned.1.call-update) | async-done | bytes 2097168 | tf_op jit(solution)/shard_map/all_gather | solution.py:83
  141.1 2.5 broadcast_in_dim.58
  143.6 27.1 %while.20 = (s32[]{:T(128)}, f32[128,512]{0,1:T(8,128)S(1)}, f32[128,512]{0,1:T(8,128)S(1)}, f32[2048,512]{0,1:T(8,128)}, s32[16,1]{0,1:T(1,128)S(1)}, /*index=5...) while((s32[]{:T(128)}, f32[128,512]{0,1:T(8,128)S(1)}, ...), condition=%wide.region_8.9_spmd.clone, body=%wide.region_3.8_spmd.clone.sunk | while | flops 691094656 | bytes 72766960 | solution.py:118
  145.4 11.8 %conditional.3 = ((f32[128,512]{0,1:T(8,128)S(1)}, f32[128,512]{0,1:T(8,128)S(1)}, f32[2048,512]{0,1:T(8,128)})) conditional(s32[]{:T(128)} %convert_element_type.86, (f32[128,512]{0,1:T(8,128)S(1)}, f32[128,512]{0,1:T(8,128)S(1)}, f32[2048,512]{0,1:T(8,128)}) %tuple.80, (s32[]{:T(128)}, bf16[2048,512]{0,1:T(8,128)(2,1)}, ...), branch_computations={%region_6.6_spmd, %region_7.7_spmd} | conditional | flops 690356224 | bytes 72220808 | solution.py:116
  148.9 1.4 fusion.4
  150.3 2.4 multiply_convert_fusion.1
  155.2 1.9 copy-done.2
  158.9 11.8 %conditional.3 = ((f32[128,512]{0,1:T(8,128)S(1)}, f32[128,512]{0,1:T(8,128)S(1)}, f32[2048,512]{0,1:T(8,128)})) conditional(s32[]{:T(128)} %convert_element_type.86, (f32[128,512]{0,1:T(8,128)S(1)}, f32[128,512]{0,1:T(8,128)S(1)}, f32[2048,512]{0,1:T(8,128)}) %tuple.80, (s32[]{:T(128)}, bf16[2048,512]{0,1:T(8,128)(2,1)}, ...), branch_computations={%region_6.6_spmd, %region_7.7_spmd} | conditional | flops 690356224 | bytes 72220808 | solution.py:116
  162.4 1.4 fusion.4
  163.9 2.4 multiply_convert_fusion.1
  168.7 1.9 copy-done.2
  176.0 14.4 %all-to-all-start = ((s32[32,1,8]{2,1,0:T(1,128)}), s32[32,1,8]{2,1,0:T(1,128)S(1)}, u32[]{:S(2)}, u32[]{:S(2)}) async-start(s32[32,1,8]{2,1,0:T(1,128)} %bitcast.14), calls=%async_computation | async-start | bytes 32768 | tf_op jit(solution)/shard_map/all_to_all | solution.py:147
  190.4 72.2 %reduce-scatter.2.cloned.1.call-done = f32[128,512]{0,1:T(8,128)} async-done(((f32[2048,512]{0,1:T(8,128)}), f32[128,512]{0,1:T(8,128)}) %reduce-scatter.2.cloned.1.call-update) | async-done | bytes 262160 | tf_op jit(solution)/shard_map/reduce_scatter | solution.py:121
  264.2 1.7 scatter_custom_fusion.1
  265.9 14.8 %all-to-all-start.1 = ((bf16[32,8,512]{2,1,0:T(8,128)(2,1)}), bf16[32,8,512]{2,1,0:T(8,128)(2,1)S(1)}, u32[]{:S(2)}, u32[]{:S(2)}) async-start(bf16[32,8,512]{2,1,0:T(8,128)(2,1)} %bitcast.17), calls=%async_computation.2 | async-start | bytes 524288 | tf_op jit(solution)/shard_map/all_to_all | solution.py:146
  282.2 20.8 %all-to-all-done.1 = bf16[32,8,512]{2,1,0:T(8,128)(2,1)S(1)} async-done(((bf16[32,8,512]{2,1,0:T(8,128)(2,1)}), bf16[32,8,512]{2,1,0:T(8,128)(2,1)S(1)}, u32[]{:S(2)}, u32[]{:S(2)}) %all-to-all-start.1) | async-done | bytes 262176 | tf_op jit(solution)/shard_map/all_to_all | solution.py:146
  304.4 103.3 %all-reduce.2.cloned.1.call-done = bf16[512,512]{1,0:T(8,128)(2,1)} async-done(((bf16[512,512]{1,0:T(8,128)(2,1)}), bf16[512,512]{1,0:T(8,128)(2,1)}) %all-reduce.2.cloned.1.call-update) | async-done | bytes 524304 | tf_op jit(solution)/shard_map/psum | solution.py:152
  409.6 2.5 subtract_convert_fusion
  414.0 15.0 %all-to-all-start.2 = ((bf16[32,8,512]{2,1,0:T(8,128)(2,1)}), bf16[32,8,512]{2,1,0:T(8,128)(2,1)S(1)}, u32[]{:S(2)}, u32[]{:S(2)}) async-start(bf16[32,8,512]{2,1,0:T(8,128)(2,1)} %bitcast_select_fusion), calls=%async_computation.3 | async-start | bytes 524288 | tf_op jit(solution)/shard_map/all_to_all | solution.py:158
  429.0 22.2 %all-to-all-done.2 = bf16[32,8,512]{2,1,0:T(8,128)(2,1)S(1)} async-done(((bf16[32,8,512]{2,1,0:T(8,128)(2,1)}), bf16[32,8,512]{2,1,0:T(8,128)(2,1)S(1)}, u32[]{:S(2)}, u32[]{:S(2)}) %all-to-all-start.2) | async-done | bytes 262176 | tf_op jit(solution)/shard_map/all_to_all | solution.py:158
  451.3 1.5 gather_fusion.3
  (95 shorter events, 32.2 us)
Async XLA Ops:
  7.2 1.4 copy-start
  7.2 68.4 %all-gather.4.cloned.1.call-start = ((), (), s32[]{:S(2)}) async-start(), calls=%async_computation.4 | async-start | bytes 2228224 | tf_op jit(solution)/shard_map/all_gather | solution.py:82
  10.6 130.5 %all-gather.6.cloned.1.call-start = ((), (), s32[]{:S(2)}) async-start(), calls=%async_computation.7 | async-start | bytes 2228224 | tf_op jit(solution)/shard_map/all_gather | solution.py:83
  12.3 250.2 %reduce-scatter.2.cloned.1.call-start = ((), (), s32[]{:S(2)}) async-start(), calls=%async_computation.5 | async-start | bytes 4456448 | tf_op jit(solution)/shard_map/reduce_scatter | solution.py:121
  152.7 2.2 copy-start.1
  155.2 2.0 copy-start.2
  166.2 2.2 copy-start.1
  168.7 2.0 copy-start.2
  170.7 0.7 copy-start.8
  170.7 0.9 copy-start.4
  170.7 2.3 copy-start.5
  171.3 237.6 %copy-start.7 = (f32[512]{0:T(512)S(1)}, f32[512]{0:T(512)}, u32[]{:S(2)}) copy-start(f32[512]{0:T(512)} %param.23) | copy-start | bytes 6148
  171.3 238.2 %copy-start.6 = (f32[512,512]{1,0:T(8,128)S(1)}, f32[512,512]{1,0:T(8,128)}, u32[]{:S(2)}) copy-start(f32[512,512]{1,0:T(8,128)} %param.22) | copy-start | bytes 3145732
  176.0 89.9 %all-to-all-start = ((s32[32,1,8]{2,1,0:T(1,128)}), s32[32,1,8]{2,1,0:T(1,128)S(1)}, u32[]{:S(2)}, u32[]{:S(2)}) async-start(s32[32,1,8]{2,1,0:T(1,128)} %bitcast.14), calls=%async_computation | async-start | bytes 32768 | tf_op jit(solution)/shard_map/all_to_all | solution.py:147
  265.9 37.1 %all-to-all-start.1 = ((bf16[32,8,512]{2,1,0:T(8,128)(2,1)}), bf16[32,8,512]{2,1,0:T(8,128)(2,1)S(1)}, u32[]{:S(2)}, u32[]{:S(2)}) async-start(bf16[32,8,512]{2,1,0:T(8,128)(2,1)} %bitcast.17), calls=%async_computation.2 | async-start | bytes 524288 | tf_op jit(solution)/shard_map/all_to_all | solution.py:146
  280.7 127.0 %all-reduce.2.cloned.1.call-start = ((), (), s32[]{:S(2)}) async-start(), calls=%async_computation.6 | async-start | bytes 1048576 | tf_op jit(solution)/shard_map/psum | solution.py:152
  412.1 40.7 %copy-start.3 = (bf16[512,512]{1,0:T(8,128)(2,1)}, bf16[512,512]{1,0:T(8,128)(2,1)S(1)}, u32[]{:S(2)}) copy-start(bf16[512,512]{1,0:T(8,128)(2,1)S(1)} %get-tuple-element.535) | copy-start | bytes 1572868
  414.0 37.2 %all-to-all-start.2 = ((bf16[32,8,512]{2,1,0:T(8,128)(2,1)}), bf16[32,8,512]{2,1,0:T(8,128)(2,1)S(1)}, u32[]{:S(2)}, u32[]{:S(2)}) async-start(bf16[32,8,512]{2,1,0:T(8,128)(2,1)} %bitcast_select_fusion), calls=%async_computation.3 | async-start | bytes 524288 | tf_op jit(solution)/shard_map/all_to_all | solution.py:158
Sparse Core Ops, SparseCore 0:
  11.6 63.9 all-gather.3
  79.1 61.9 all-gather.5
  170.8 91.6 reduce-scatter.1
  304.3 103.4 all-reduce.1
where the time goes:
time: 460 us; the launch traced here: 459 us
  waiting for transfers between devices  342 us (74%)
  starting transfers between devices  44.3 us (10%)
  local copies, waits for them, and re-layouts  32.5 us (7%)
  matrix products  14.9 us (3%)
  between operations  14 us (3%)
  other arithmetic  9.82 us (2%)
    psum x1, waiting for transfers between devices, body(): lax.psum(slab_grad.astype(jnp.bfloat16), 'seq').astype(jnp.float32)  103 us
    reduce_scatter x1, waiting for transfers between devices, body(): lax.psum_scatter(query_terms, 'seq', scatter_dimension=0, tiled=True)  72.2 us
    all_gather x1, waiting for transfers between devices, body(): query_piece = lax.all_gather(queries, 'seq', axis=0, tiled=True)  62.1 us
    all_gather x1, waiting for transfers between devices, body(): grad_piece = lax.all_gather(cotangent, 'seq', axis=0, tiled=True)  61.6 us
    all_to_all x1, waiting for transfers between devices, body(): lax.all_to_all(replies, 'table', split_axis=0, concat_axis=0, tiled=True)  22.2 us
    all_to_all x1, waiting for transfers between devices, body(): lax.all_to_all(send_rows, 'table', split_axis=0, concat_axis=0, tiled=True)  20.8 us
    all_to_all x1, starting transfers between devices, body(): lax.all_to_all(replies, 'table', split_axis=0, concat_axis=0, tiled=True)  15 us
    all_to_all x1, starting transfers between devices, body(): lax.all_to_all(send_rows, 'table', split_axis=0, concat_axis=0, tiled=True)  14.8 us
  transfers between devices with their start and end apart: 7, of which 6 were waited for; matrix products, arithmetic and copies ran while one was open for 3% of the time, Pallas kernels for 0%

commit v1 on v0

v1 whole, which is shorter than its diff:
```python
import math

import jax
import jax.numpy as jnp
from jax import lax
from jax.experimental import pallas as pl
from jax.experimental.pallas import tpu as pltpu
from jax.sharding import PartitionSpec as P

HEADS = 8
LANES = 128
DIGIT = 16

first_decay = 0.9
second_decay = 0.99
step_rate = 0.05
epsilon = 1e-08

f32 = jnp.float32
bf16 = jnp.bfloat16


def swap_halves(block):
    half = block.shape[1] // 2
    return pltpu.roll(block, half, 1)


def low_lanes(shape):
    return lax.broadcasted_iota(jnp.int32, shape, 1) < shape[1] // 2


def pair_low(first, second):
    return jnp.where(low_lanes(first.shape), first, swap_halves(second))


def pair_high(first, second):
    return jnp.where(low_lanes(first.shape), swap_halves(first), second)


def project_kernel(x_ref, proj_ref, grad_ref, send_ref):
    features = x_ref.shape[1]
    rows = x_ref.shape[0]
    half = rows // 2
    x = x_ref[...]
    for pair in range(HEADS // 2):
        at = pair * LANES
        parts = [
            jnp.dot(
                x, proj_ref[:, third * features + at : third * features + at + LANES],
                preferred_element_type=f32,
            )
            for third in range(3)
        ]
        cot = grad_ref[:, at : at + LANES].astype(f32)
        queries, keys, values = parts
        for odd, join in ((0, pair_low), (1, pair_high)):
            query_grad = join(queries, cot).astype(bf16)
            key_value = join(keys, values).astype(bf16)
            for part in range(2):
                slot = 2 * (2 * pair + odd) + part
                send_ref[slot, 0:rows, :] = query_grad
                send_ref[slot, rows : rows + half, :] = key_value[part * half : part * half + half]


def attention_kernel(part_ref, seen_ref, got_ref, out_ref, key_s, value_s, total_s):
    blocks = got_ref.shape[0]
    rows = out_ref.shape[1]
    half = rows // 2
    tile = 2 * rows
    history_scale = 1.0 / math.sqrt(rows * blocks)
    part = part_ref[0]
    both = got_ref[:, rows : rows + half, :].reshape(blocks * half, LANES)
    low = low_lanes(both.shape)
    zero = jnp.zeros_like(both)
    key_s[...] = jnp.where(low, both * jnp.bfloat16(0.0625), zero)
    value_s[...] = jnp.where(low, zero, both)
    key_row = lax.broadcasted_iota(jnp.int32, (rows, tile), 0)
    query_col = lax.broadcasted_iota(jnp.int32, (rows, tile), 1)
    key_pos = (key_row // half) * rows + part * half + key_row % half
    causal = (key_pos <= query_col).astype(f32)
    for step in range(blocks // 2):
        query_grad = got_ref[2 * step : 2 * step + 2, 0:rows, :].reshape(tile, LANES)
        query_total = jnp.zeros((tile, LANES), f32)
        for chunk in range(step + 1):
            keys = key_s[chunk * rows : chunk * rows + rows, :]
            values = value_s[chunk * rows : chunk * rows + rows, :]
            half_scores = lax.dot_general(
                keys, query_grad, (((1,), (1,)), ((), ())), preferred_element_type=f32
            )
            weight_grad = lax.dot_general(
                values, query_grad, (((1,), (1,)), ((), ())), preferred_element_type=f32
            )
            seen = jnp.concatenate(
                [
                    jnp.broadcast_to(
                        seen_ref[2 * chunk + b : 2 * chunk + b + 1, step * tile : step * tile + tile],
                        (half, tile),
                    )
                    for b in range(2)
                ],
                axis=0,
            )
            if chunk == step:
                seen = seen * causal
            gate2 = (1.0 + jnp.tanh(half_scores)) * seen
            weights = half_scores * gate2
            score_grad = (weight_grad * (gate2 + weights * (2.0 - gate2))).astype(bf16)
            weights = weights.astype(bf16)
            key_part = jnp.dot(score_grad, query_grad, preferred_element_type=f32)
            value_part = jnp.dot(weights, query_grad, preferred_element_type=f32)
            joined = jnp.where(low_lanes(key_part.shape), key_part, value_part)
            if chunk == step:
                total_s[chunk * rows : chunk * rows + rows, :] = joined
            else:
                total_s[chunk * rows : chunk * rows + rows, :] += joined
            query_total += lax.dot_general(
                score_grad, keys, (((0,), (0,)), ((), ())), preferred_element_type=f32
            )
        query_total = query_total * history_scale
        for b in range(2):
            top = query_total[b * rows : b * rows + half]
            bottom = query_total[b * rows + half : b * rows + rows]
            out_ref[2 * step + b, half:rows, :] = (top + swap_halves(bottom)).astype(bf16)
    scale = jnp.where(low_lanes((1, LANES)), history_scale * 0.0625, history_scale)
    out_ref[:, 0:half, :] = (total_s[...] * scale).astype(bf16).reshape(blocks, half, LANES)


def input_grad_kernel(got_ref, proj_ref, target_ref, digits_ref, send_ref):
    rows = got_ref.shape[1]
    half = rows // 2
    queries, keys, values = [], [], []
    for pair in range(HEADS // 2):
        query, joint = [], []
        for odd in range(2):
            slot = 2 * (2 * pair + odd)
            query.append(
                got_ref[slot, half:rows, :].astype(f32) + got_ref[slot + 1, half:rows, :].astype(f32)
            )
            joint.append(
                jnp.concatenate(
                    [got_ref[slot, 0:half, :], got_ref[slot + 1, 0:half, :]], axis=0
                ).astype(f32)
            )
        queries.append(jnp.concatenate([pair_low(*query), pair_high(*query)], axis=0))
        keys.append(pair_low(*joint))
        values.append(pair_high(*joint))
    stacked = jnp.concatenate(queries + keys + values, axis=1).astype(bf16)
    input_grad = lax.dot_general(
        stacked, proj_ref[...], (((1,), (1,)), ((), ())), preferred_element_type=f32
    ).astype(bf16)
    slots = send_ref.shape[0]
    features = input_grad.shape[1]
    onehot = (
        lax.broadcasted_iota(jnp.int32, (slots, rows), 0) == target_ref[...]
    ).astype(f32).astype(bf16)
    send_ref[:, 0:features] = jnp.dot(onehot, input_grad, preferred_element_type=f32).astype(bf16)
    send_ref[:, features:] = jnp.dot(onehot, digits_ref[...], preferred_element_type=f32).astype(bf16)


def slot_rows(digits, slab_rows):
    digits = digits.astype(f32)
    row = digits[:, 0:1] * DIGIT + digits[:, 1:2] - DIGIT
    lane = lax.broadcasted_iota(jnp.int32, (digits.shape[0], slab_rows), 1).astype(f32)
    return (row == lane).astype(f32).astype(bf16)


def slab_kernel(got_ref, slab_ref):
    slab_rows, features = slab_ref.shape
    select = slot_rows(got_ref[:, features:], slab_rows)
    slab_ref[...] = lax.dot_general(
        select, got_ref[:, 0:features], (((0,), (0,)), ((), ())), preferred_element_type=f32
    ).astype(bf16)


def sum_kernel(got_ref, out_ref):
    count = got_ref.shape[0]
    total = got_ref[0].astype(f32)
    for source in range(1, count):
        total += got_ref[source].astype(f32)
    total = total.astype(bf16)
    for target in range(count):
        out_ref[target] = total


def adam_kernel(
    grad_ref, moment_ref, second_ref, table_ref, digits_ref,
    new_table_ref, new_moment_ref, new_second_ref, reply_ref,
):
    item_grad = grad_ref[...].astype(f32)
    new_moment = first_decay * moment_ref[...] + (1.0 - first_decay) * item_grad
    new_moment_ref[...] = new_moment
    mean = jnp.mean(item_grad * item_grad, axis=1, keepdims=True)
    new_second = second_decay * second_ref[...] + (1.0 - second_decay) * mean
    new_second_ref[...] = new_second
    new_table = (
        table_ref[...].astype(f32) - step_rate * new_moment / (jnp.sqrt(new_second) + epsilon)
    ).astype(bf16)
    new_table_ref[...] = new_table
    select = slot_rows(digits_ref[...], new_table.shape[0])
    reply_ref[...] = jnp.dot(select, new_table, preferred_element_type=f32).astype(bf16)


def event_kernel(target_ref, got_ref, out_ref):
    slots = got_ref.shape[0]
    rows = out_ref.shape[0]
    onehot = (
        lax.broadcasted_iota(jnp.int32, (slots, rows), 0) == target_ref[...]
    ).astype(f32).astype(bf16)
    out_ref[...] = lax.dot_general(
        onehot, got_ref[...], (((0,), (0,)), ((), ())), preferred_element_type=f32
    ).astype(bf16)


def shape(dims, kind):
    return jax.ShapeDtypeStruct(dims, kind)


def exchange(array, axis):
    return lax.all_to_all(array, axis, split_axis=0, concat_axis=0, tiled=True)


def body(events_x, proj, out_grad, block_mask, item_ids, owner_of, local_of, table, moment, second):
    tokens = events_x.shape[1]
    features = events_x.shape[2]
    seq_count = lax.axis_size("seq")
    owner_count = lax.axis_size("table")
    position = lax.axis_index("seq")
    slab_rows = table.shape[0]
    capacity = 2 * tokens // owner_count
    slots = owner_count * capacity
    half = tokens // 2

    send = pl.pallas_call(
        project_kernel,
        out_shape=shape((seq_count, tokens + half, LANES), bf16),
        name="project",
    )(events_x[0], proj, out_grad[0])
    got = exchange(send, "seq")

    block_ids = jnp.arange(seq_count)
    query_blk = jnp.arange(seq_count * tokens) // tokens
    visible = (block_mask == 1) | (block_ids[:, None] == block_ids[None, :])
    seen = jnp.repeat(visible.T.astype(f32), tokens, axis=1)
    part = (position % 2).astype(jnp.int32).reshape(1)
    back = pl.pallas_call(
        attention_kernel,
        out_shape=shape((seq_count, tokens, LANES), bf16),
        in_specs=[
            pl.BlockSpec(memory_space=pltpu.SMEM),
            pl.BlockSpec(memory_space=pltpu.VMEM),
            pl.BlockSpec(memory_space=pltpu.VMEM),
        ],
        scratch_shapes=[
            pltpu.VMEM((seq_count * half, LANES), bf16),
            pltpu.VMEM((seq_count * half, LANES), bf16),
            pltpu.VMEM((seq_count * half, LANES), f32),
        ],
        name="attention",
    )(part, seen, got)
    got_back = exchange(back, "seq")

    place_of = owner_of * slab_rows + local_of
    place = place_of[item_ids[0]]
    owners = place // slab_rows
    slab_index = place % slab_rows
    event = jnp.arange(tokens)
    earlier = (owners[:, None] == owners[None, :]) & (event[:, None] < event[None, :])
    rank = jnp.sum(earlier.astype(jnp.int32), axis=0)
    target = (owners * capacity + rank)[None, :]
    lane = jnp.arange(LANES)[None, :]
    digits = jnp.where(
        lane == 0,
        (slab_index // DIGIT + 1)[:, None],
        jnp.where(lane == 1, (slab_index % DIGIT)[:, None], 0),
    ).astype(bf16)
    send_rows = pl.pallas_call(
        input_grad_kernel,
        out_shape=shape((slots, features + LANES), bf16),
        name="input_grad",
    )(got_back, proj, target, digits)
    got_rows = exchange(
        send_rows.reshape(owner_count, capacity, features + LANES), "table"
    ).reshape(slots, features + LANES)

    slab = pl.pallas_call(slab_kernel, out_shape=shape((slab_rows, features), bf16), name="slab")(
        got_rows
    )
    share = slab_rows // seq_count
    parts = exchange(slab.reshape(seq_count, share, features), "seq")
    copies = pl.pallas_call(
        sum_kernel, out_shape=shape((seq_count, share, features), bf16), name="row_sum"
    )(parts)
    item_grad = exchange(copies, "seq").reshape(slab_rows, features)

    new_table, new_moment, new_second, reply = pl.pallas_call(
        adam_kernel,
        out_shape=(
            shape((slab_rows, features), bf16),
            shape((slab_rows, features), f32),
            shape((slab_rows, 1), f32),
            shape((slots, features), bf16),
        ),
        name="adam",
    )(item_grad, moment, second[:, None], table, got_rows[:, features:])
    returned = exchange(reply.reshape(owner_count, capacity, features), "table")
    event_rows = pl.pallas_call(
        event_kernel, out_shape=shape((tokens, features), bf16), name="event_rows"
    )(target, returned.reshape(slots, features))
    return (new_table, new_moment, new_second[:, 0], event_rows[None])


def solution(mesh):
    return jax.shard_map(
        body,
        mesh=mesh,
        in_specs=(
            P("table", "seq", None),
            P(),
            P("table", "seq", None),
            P(),
            P("table", "seq"),
            P(),
            P(),
            P("table", None),
            P("table", None),
            P("table"),
        ),
        out_specs=(P("table", None), P("table", None), P("table"), P("table", "seq", None)),
        check_vma=False,
    )
```

time: 460 us -> 164 us (0.36)
  waiting for transfers between devices: 342 us -> 44.9 us
  blocking collectives: 0 us -> 60.4 us
  Pallas kernels: 0 us -> 25.2 us
  local copies, waits for them, and re-layouts: 32.5 us -> 7.54 us
  starting transfers between devices: 44.3 us -> 20.9 us
  matrix products: 14.9 us -> 0 us
  between operations: 14 us -> 0.79 us
  other arithmetic: 9.82 us -> 3.11 us
    all_gather x2 -> x0, waiting for transfers between devices: 124 us -> none  [the longest x1 62.1 us: body(): query_piece = lax.all_gather(queries, 'seq', axis=0, tiled=True)]
    psum x1 -> x0, waiting for transfers between devices: 103 us -> none  [body(): lax.psum(slab_grad.astype(jnp.bfloat16), 'seq').astype(jnp.float32)]
    reduce_scatter x1 -> x0, waiting for transfers between devices: 72.2 us -> none  [body(): lax.psum_scatter(query_terms, 'seq', scatter_dimension=0, tiled=True)]
    all_to_all x0 -> x2, blocking collectives: none -> 60.4 us  [exchange(): return lax.all_to_all(array, axis, split_axis=0, concat_axis=0, tiled=True)]
    pallas_call x0 -> x7, Pallas kernels: none -> 25.2 us  [the longest x1 9.66 us: body(): pl.pallas_call(attention_kernel, out_shape=shape((seq_count, tokens, LANE...]
    all_to_all x3 -> x4, starting transfers between devices: 44.1 us -> 20.9 us  [exchange(): return lax.all_to_all(array, axis, split_axis=0, concat_axis=0, tiled=True)]
    dot_general x13 -> x0, matrix products: 14.9 us -> none  [the longest x2 4.71 us: pair_terms(): jnp.einsum('qhe,khe->hqk', split_heads(grad_block), split_heads(value_blo...]
    dynamic_slice x5 -> x0, local copies, waits for them, and re-layouts: 5.97 us -> none  [the longest x2 2.6 us: advance(): lax.dynamic_slice_in_dim(query_piece, first_row, block_rows, 0)]
  transfers between devices with their start and end apart: 7 -> 4, of which waited for: 6 -> 4; matrix products, arithmetic and copies ran while one was open for 3% -> 5% of each run, Pallas kernels for 0% -> 0%
where the time goes in v1:
time: 164 us; the launch traced here: 163 us
  blocking collectives  60.4 us (37%)
  waiting for transfers between devices  44.9 us (27%)
  Pallas kernels  25.2 us (15%)
  starting transfers between devices  20.9 us (13%)
  local copies, waits for them, and re-layouts  7.54 us (5%)
  other arithmetic  3.11 us (2%)
    all_to_all x2, blocking collectives, exchange(): return lax.all_to_all(array, axis, split_axis=0, concat_axis=0, tiled=True)  60.4 us
    all_to_all x4, waiting for transfers between devices, exchange(): return lax.all_to_all(array, axis, split_axis=0, concat_axis=0, tiled=True)  44.9 us
    all_to_all x4, starting transfers between devices, exchange(): return lax.all_to_all(array, axis, split_axis=0, concat_axis=0, tiled=True)  20.9 us
    pallas_call x1, Pallas kernels, body(): pl.pallas_call(attention_kernel, out_shape=shape((seq_count, tokens, LANE...  9.66 us
    unnamed x19, local copies, waits for them, and re-layouts  3.9 us
    pallas_call x1, Pallas kernels, body(): pl.pallas_call(adam_kernel, out_shape=(shape((slab_rows, features), bf16)...  3.47 us
  transfers between devices with their start and end apart: 4, of which 4 were waited for; matrix products, arithmetic and copies ran while one was open for 5% of the time, Pallas kernels for 0%

profile of v1, /device:TPU:1, one launch (start us, length us, event | category | flops | bytes accessed | tf_op | source)
XLA Modules:
  0.0 162.8 jit_solution(7475417775263889953)
XLA Ops:
  0.7 3.0 %project.1 = bf16[16,192,128]{2,1,0:T(8,128)(2,1)} custom-call(bf16[128,512]{1,0:T(8,128)(2,1)} %bitcast.42, bf16[512,1536]{1,0:T(8,128)(2,1)} %proj_ref.3, bf16[128,512]{1,0:T(8,128)(2,1)} %bitcast.43), custom_call_target="tpu_custom_call" | custom-call | tf_op jit(solution)/shard_map/project/pallas_call | solution.py:233
  3.6 7.7 %all-to-all-start = ((bf16[16,192,128]{2,1,0:T(8,128)(2,1)}), bf16[16,192,128]{2,1,0:T(8,128)(2,1)S(1)}, u32[]{:S(2)}, u32[]{:S(2)}) async-start(bf16[16,192,128]{2,1,0:T(8,128)(2,1)} %project.1), calls=%async_computation | async-start | bytes 1572864 | tf_op jit(solution)/shard_map/all_to_all | solution.py:219
  12.3 1.1 gather_fusion
  13.6 9.5 %all-to-all-done.got_ref = bf16[16,192,128]{2,1,0:T(8,128)(2,1)S(1)} async-done(((bf16[16,192,128]{2,1,0:T(8,128)(2,1)}), bf16[16,192,128]{2,1,0:T(8,128)(2,1)S(1)}, u32[]{:S(2)}, u32[]{:S(2)}) %all-to-all-start) | async-done | bytes 786464 | tf_op jit(solution)/shard_map/all_to_all | solution.py:219
  23.1 0.9 copy-done
  24.0 9.7 %attention.1 = bf16[16,128,128]{2,1,0:T(8,128)(2,1)} custom-call(s32[1]{0:T(128)} %bitcast.part_ref, f32[16,2048]{1,0:T(8,128)} %bitcast.40, bf16[16,192,128]{2,1,0:T(8,128)(2,1)} %copy-done), custom_call_target="tpu_custom_call" | custom-call | tf_op jit(solution)/shard_map/attention/pallas_call | solution.py:245
  33.6 3.6 %all-to-all-start.1 = ((bf16[16,128,128]{2,1,0:T(8,128)(2,1)}), bf16[16,128,128]{2,1,0:T(8,128)(2,1)S(1)}, u32[]{:S(2)}, u32[]{:S(2)}) async-start(bf16[16,128,128]{2,1,0:T(8,128)(2,1)} %attention.1), calls=%async_computation.1 | async-start | bytes 1048576 | tf_op jit(solution)/shard_map/all_to_all | solution.py:219
  38.5 7.8 %all-to-all-done.1.got_ref = bf16[16,128,128]{2,1,0:T(8,128)(2,1)S(1)} async-done(((bf16[16,128,128]{2,1,0:T(8,128)(2,1)}), bf16[16,128,128]{2,1,0:T(8,128)(2,1)S(1)}, u32[]{:S(2)}, u32[]{:S(2)}) %all-to-all-start.1) | async-done | bytes 524320 | tf_op jit(solution)/shard_map/all_to_all | solution.py:219
  46.3 0.8 copy-done.2
  47.1 3.1 %input_grad.1 = bf16[256,640]{1,0:T(8,128)(2,1)} custom-call(bf16[16,128,128]{2,1,0:T(8,128)(2,1)} %copy-done.2, bf16[512,1536]{1,0:T(8,128)(2,1)} %proj_ref.3, s32[1,128]{1,0:T(1,128)} %bitcast_add_fusion.target_ref, bf16[128,128]{1,0:T(8,128)(2,1)} %select_convert_fusion.digits_ref), custom_call_target="tpu_custom_call" | custom-call | tf_op jit(solution)/shard_map/input_grad/pallas_call | solution.py:276
  50.2 45.4 %all_to_all.30 = bf16[32,8,640]{2,1,0:T(8,128)(2,1)} all-to-all(bf16[32,8,640]{2,1,0:T(8,128)(2,1)} %bitcast.37), channel_id=1, replica_groups=mesh['seq'=16,'table'=32] {'table'}, dimensions={0} | all-to-all | bytes 655360 | tf_op jit(solution)/shard_map/all_to_all | solution.py:219
  95.6 2.3 %slab.1 = bf16[512,512]{1,0:T(8,128)(2,1)} custom-call(bf16[256,640]{1,0:T(8,128)(2,1)} %bitcast.35), custom_call_target="tpu_custom_call" | custom-call | tf_op jit(solution)/shard_map/slab/pallas_call | solution.py:285
  97.8 15.0 %all_to_all.31.got_ref = bf16[16,32,512]{2,1,0:T(8,128)(2,1)} all-to-all(bf16[16,32,512]{2,1,0:T(8,128)(2,1)} %bitcast.34), channel_id=1, replica_groups=mesh['seq'=16,'table'=32] {'seq'}, dimensions={0} | all-to-all | bytes 1048576 | tf_op jit(solution)/shard_map/all_to_all | solution.py:219
  112.8 1.9 %row_sum.1 = bf16[16,32,512]{2,1,0:T(8,128)(2,1)} custom-call(bf16[16,32,512]{2,1,0:T(8,128)(2,1)} %all_to_all.31.got_ref), custom_call_target="tpu_custom_call" | custom-call | tf_op jit(solution)/shard_map/row_sum/pallas_call | solution.py:290
  114.8 3.6 %all-to-all-start.4 = ((bf16[16,32,512]{2,1,0:T(8,128)(2,1)}), bf16[16,32,512]{2,1,0:T(8,128)(2,1)S(1)}, u32[]{:S(2)}, u32[]{:S(2)}) async-start(bf16[16,32,512]{2,1,0:T(8,128)(2,1)} %row_sum.1), calls=%async_computation.4 | async-start | bytes 1048576 | tf_op jit(solution)/shard_map/all_to_all | solution.py:219
  118.4 0.9 copy.18.second_ref
  119.2 1.5 slice.6.digits_ref
  120.7 7.6 %all-to-all-done.4 = bf16[16,32,512]{2,1,0:T(8,128)(2,1)S(1)} async-done(((bf16[16,32,512]{2,1,0:T(8,128)(2,1)}), bf16[16,32,512]{2,1,0:T(8,128)(2,1)S(1)}, u32[]{:S(2)}, u32[]{:S(2)}) %all-to-all-start.4) | async-done | bytes 524320 | tf_op jit(solution)/shard_map/all_to_all | solution.py:219
  128.3 0.8 copy-done.1
  129.2 3.5 %adam.1 = (bf16[512,512]{1,0:T(8,128)(2,1)}, f32[512,512]{1,0:T(8,128)}, f32[512,1]{1,0:T(8,128)}, bf16[256,512]{1,0:T(8,128)(2,1)}) custom-call(bf16[512,512]{1,0:T(8,128)(2,1)} %bitcast.33, f32[512,512]{1,0:T(8,128)} %moment_ref.1, f32[512,1]{1,0:T(8,128)} %copy.18.second_ref, bf16[512,512]{1,0:T(8,128)(2,1)} %table_ref.1, bf16[256,128]{1,0:T(8,128)(2,1)} %slice.6.digits_ref), custom_call_target="tpu_custom_call" | custom-call | tf_op jit(solution)/shard_map/adam/pallas_call | solution.py:295
  132.6 6.0 %all-to-all-start.5 = ((bf16[32,8,512]{2,1,0:T(8,128)(2,1)}), bf16[32,8,512]{2,1,0:T(8,128)(2,1)S(1)}, u32[]{:S(2)}, u32[]{:S(2)}) async-start(bf16[32,8,512]{2,1,0:T(8,128)(2,1)} %bitcast.41), calls=%async_computation.5 | async-start | bytes 524288 | tf_op jit(solution)/shard_map/all_to_all | solution.py:219
  138.7 1.7 %reduce = f32[512]{0:T(512)} reduce(f32[512,1]{1,0:T(8,128)} %get-tuple-element.10, f32[]{:T(128)} %constant.79), dimensions={1}, to_apply=%get-tuple-element.10.reduce_sub_computation | reduce | bytes 4100 | tf_op jit(solution)/shard_map/adam/pallas_call | solution.py:295
  140.3 20.0 %all-to-all-done.5 = bf16[32,8,512]{2,1,0:T(8,128)(2,1)S(1)} async-done(((bf16[32,8,512]{2,1,0:T(8,128)(2,1)}), bf16[32,8,512]{2,1,0:T(8,128)(2,1)S(1)}, u32[]{:S(2)}, u32[]{:S(2)}) %all-to-all-start.5) | async-done | bytes 262176 | tf_op jit(solution)/shard_map/all_to_all | solution.py:219
  161.0 1.8 %event_rows.1 = bf16[128,512]{1,0:T(8,128)(2,1)} custom-call(s32[1,128]{1,0:T(1,128)} %bitcast_add_fusion.target_ref, bf16[256,512]{1,0:T(8,128)(2,1)} %bitcast.38), custom_call_target="tpu_custom_call" | custom-call | tf_op jit(solution)/shard_map/event_rows/pallas_call | solution.py:306
  (29 shorter events, 3.0 us)
Async XLA Ops:
  0.6 10.7 %copy-start.8 = (s32[1,128]{1,0:T(1,128)S(1)}, s32[1,128]{1,0:T(1,128)}, u32[]{:S(2)}) copy-start(s32[1,128]{1,0:T(1,128)} %param.14) | copy-start | bytes 1540
  0.6 10.7 %copy-start.6 = (s32[16,16]{1,0:T(8,128)S(1)}, s32[16,16]{1,0:T(8,128)}, u32[]{:S(2)}) copy-start(s32[16,16]{1,0:T(8,128)} %param.13) | copy-start | bytes 3076
  3.6 8.7 %copy-start.4 = (s32[16384]{0:T(1024)S(1)}, s32[16384]{0:T(1024)}, u32[]{:S(2)}) copy-start(s32[16384]{0:T(1024)} %param.16) | copy-start | bytes 196612
  3.6 8.7 %copy-start.5 = (s32[16384]{0:T(1024)S(1)}, s32[16384]{0:T(1024)}, u32[]{:S(2)}) copy-start(s32[16384]{0:T(1024)} %param.15) | copy-start | bytes 196612
  3.6 19.5 %all-to-all-start = ((bf16[16,192,128]{2,1,0:T(8,128)(2,1)}), bf16[16,192,128]{2,1,0:T(8,128)(2,1)S(1)}, u32[]{:S(2)}, u32[]{:S(2)}) async-start(bf16[16,192,128]{2,1,0:T(8,128)(2,1)} %project.1), calls=%async_computation | async-start | bytes 1572864 | tf_op jit(solution)/shard_map/all_to_all | solution.py:219
  23.1 0.9 copy-start
  33.6 12.6 %all-to-all-start.1 = ((bf16[16,128,128]{2,1,0:T(8,128)(2,1)}), bf16[16,128,128]{2,1,0:T(8,128)(2,1)S(1)}, u32[]{:S(2)}, u32[]{:S(2)}) async-start(bf16[16,128,128]{2,1,0:T(8,128)(2,1)} %attention.1), calls=%async_computation.1 | async-start | bytes 1048576 | tf_op jit(solution)/shard_map/all_to_all | solution.py:219
  46.3 0.8 copy-start.2
  97.8 20.5 %copy-start.7 = (f32[512]{0:T(512)S(1)}, f32[512]{0:T(512)}, u32[]{:S(2)}) copy-start(f32[512]{0:T(512)} %param.19) | copy-start | bytes 6148
  114.8 13.6 %all-to-all-start.4 = ((bf16[16,32,512]{2,1,0:T(8,128)(2,1)}), bf16[16,32,512]{2,1,0:T(8,128)(2,1)S(1)}, u32[]{:S(2)}, u32[]{:S(2)}) async-start(bf16[16,32,512]{2,1,0:T(8,128)(2,1)} %row_sum.1), calls=%async_computation.4 | async-start | bytes 1048576 | tf_op jit(solution)/shard_map/all_to_all | solution.py:219
  128.3 0.8 copy-start.1
  132.6 27.7 %all-to-all-start.5 = ((bf16[32,8,512]{2,1,0:T(8,128)(2,1)}), bf16[32,8,512]{2,1,0:T(8,128)(2,1)S(1)}, u32[]{:S(2)}, u32[]{:S(2)}) async-start(bf16[32,8,512]{2,1,0:T(8,128)(2,1)} %bitcast.41), calls=%async_computation.5 | async-start | bytes 524288 | tf_op jit(solution)/shard_map/all_to_all | solution.py:219
  160.3 0.7 copy-start.3

commit v2 on v1

--- a/solution.py
+++ b/solution.py
@@ -211,6 +211,14 @@
     ).astype(bf16)
 
 
+def limit(mib):
+    return pltpu.CompilerParams(vmem_limit_bytes=mib * 1024 * 1024)
+
+
+def whole(dims):
+    return pl.BlockSpec(dims, lambda i: (0, 0))
+
+
 def shape(dims, kind):
     return jax.ShapeDtypeStruct(dims, kind)
 
@@ -233,7 +241,7 @@
     send = pl.pallas_call(
         project_kernel,
         out_shape=shape((seq_count, tokens + half, LANES), bf16),
-        name="project",
+        compiler_params=limit(8), name="project",
     )(events_x[0], proj, out_grad[0])
     got = exchange(send, "seq")
 
@@ -255,7 +263,7 @@
             pltpu.VMEM((seq_count * half, LANES), bf16),
             pltpu.VMEM((seq_count * half, LANES), f32),
         ],
-        name="attention",
+        compiler_params=limit(16), name="attention",
     )(part, seen, got)
     got_back = exchange(back, "seq")
 
@@ -276,19 +284,21 @@
     send_rows = pl.pallas_call(
         input_grad_kernel,
         out_shape=shape((slots, features + LANES), bf16),
-        name="input_grad",
+        compiler_params=limit(12), name="input_grad",
     )(got_back, proj, target, digits)
     got_rows = exchange(
         send_rows.reshape(owner_count, capacity, features + LANES), "table"
     ).reshape(slots, features + LANES)
 
-    slab = pl.pallas_call(slab_kernel, out_shape=shape((slab_rows, features), bf16), name="slab")(
+    slab = pl.pallas_call(slab_kernel, out_shape=shape((slab_rows, features), bf16), compiler_params=limit(8), name="slab")(
         got_rows
     )
     share = slab_rows // seq_count
     parts = exchange(slab.reshape(seq_count, share, features), "seq")
     copies = pl.pallas_call(
-        sum_kernel, out_shape=shape((seq_count, share, features), bf16), name="row_sum"
+        sum_kernel,
+        out_shape=shape((seq_count, share, features), bf16),
+        compiler_params=limit(8), name="row_sum",
     )(parts)
     item_grad = exchange(copies, "seq").reshape(slab_rows, features)
 
@@ -300,11 +310,27 @@
             shape((slab_rows, 1), f32),
             shape((slots, features), bf16),
         ),
-        name="adam",
-    )(item_grad, moment, second[:, None], table, got_rows[:, features:])
+        grid=(1,),
+        in_specs=[
+            whole((slab_rows, features)),
+            whole((slab_rows, features)),
+            whole((slab_rows, 1)),
+            whole((slab_rows, features)),
+            pl.BlockSpec((slots, LANES), lambda i: (0, features // LANES)),
+        ],
+        out_specs=(
+            whole((slab_rows, features)),
+            whole((slab_rows, features)),
+            whole((slab_rows, 1)),
+            whole((slots, features)),
+        ),
+        compiler_params=limit(12), name="adam",
+    )(item_grad, moment, second[:, None], table, got_rows)
     returned = exchange(reply.reshape(owner_count, capacity, features), "table")
     event_rows = pl.pallas_call(
-        event_kernel, out_shape=shape((tokens, features), bf16), name="event_rows"
+        event_kernel,
+        out_shape=shape((tokens, features), bf16),
+        compiler_params=limit(8), name="event_rows",
     )(target, returned.reshape(slots, features))
     return (new_table, new_moment, new_second[:, 0], event_rows[None])
 

time: 164 us -> 152 us (0.927)
  Pallas kernels: 25.2 us -> 14.8 us
  waiting for transfers between devices: 44.9 us -> 50 us
  local copies, waits for them, and re-layouts: 7.54 us -> 4.75 us
  blocking collectives: 60.4 us -> 58.2 us
  other arithmetic: 3.11 us -> 1 us
    all_to_all x4, waiting for transfers between devices: 44.9 us -> 50 us  [exchange(): return lax.all_to_all(array, axis, split_axis=0, concat_axis=0, tiled=True)]
    pallas_call x1, Pallas kernels: 3.09 us -> 0.85 us  [body(): pl.pallas_call(input_grad_kernel, out_shape=shape((slots, features + LANE...]
    all_to_all x2, blocking collectives: 60.4 us -> 58.2 us  [exchange(): return lax.all_to_all(array, axis, split_axis=0, concat_axis=0, tiled=True)]
    pallas_call x1, Pallas kernels: 2.25 us -> 0.48 us  [body(): pl.pallas_call(slab_kernel, out_shape=shape((slab_rows, features), bf16),...]
    pallas_call x1, Pallas kernels: 3.47 us -> 1.79 us  [body(): pl.pallas_call(adam_kernel, out_shape=(shape((slab_rows, features), bf16)...]
    unnamed x19 -> x23, local copies, waits for them, and re-layouts: 3.9 us -> 3.3 us
  transfers between devices with their start and end apart: 4 -> 4, of which waited for: 4 -> 4; matrix products, arithmetic and copies ran while one was open for 5% -> 2% of each run, Pallas kernels for 0% -> 0%
where the time goes in v2:
time: 152 us
  blocking collectives  58.2 us (38%)
  waiting for transfers between devices  50 us (33%)
  starting transfers between devices  21.9 us (14%)
  Pallas kernels  14.8 us (10%)
  local copies, waits for them, and re-layouts  4.75 us (3%)
    all_to_all x2, blocking collectives, exchange(): return lax.all_to_all(array, axis, split_axis=0, concat_axis=0, tiled=True)  58.2 us
    all_to_all x4, waiting for transfers between devices, exchange(): return lax.all_to_all(array, axis, split_axis=0, concat_axis=0, tiled=True)  50 us
    all_to_all x4, starting transfers between devices, exchange(): return lax.all_to_all(array, axis, split_axis=0, concat_axis=0, tiled=True)  21.9 us
    pallas_call x1, Pallas kernels, body(): pl.pallas_call(attention_kernel, out_shape=shape((seq_count, tokens, LANE...  8.45 us
    unnamed x23, local copies, waits for them, and re-layouts  3.3 us
  transfers between devices with their start and end apart: 4, of which 4 were waited for; matrix products, arithmetic and copies ran while one was open for 2% of the time, Pallas kernels for 0%

profile of v2, /device:TPU:1, one launch (start us, length us, event | category | flops | bytes accessed | tf_op | source)
XLA Modules:
  0.0 151.6 jit_solution(4867096133342331710)
XLA Ops:
  0.6 1.4 copy-done
  2.0 0.9 copy-done.4
  2.9 0.9 copy-done.5
  3.9 1.5 %project.1 = bf16[16,192,128]{2,1,0:T(8,128)(2,1)} custom-call(bf16[128,512]{1,0:T(8,128)(2,1)S(1)} %bitcast.40, bf16[512,1536]{1,0:T(8,128)(2,1)S(1)} %copy-done, bf16[128,512]{1,0:T(8,128)(2,1)S(1)} %bitcast.41), custom_call_target="tpu_custom_call" | custom-call | tf_op jit(solution)/shard_map/project/pallas_call | solution.py:241
  5.4 7.7 %all-to-all-start = ((bf16[16,192,128]{2,1,0:T(8,128)(2,1)}), bf16[16,192,128]{2,1,0:T(8,128)(2,1)S(1)}, u32[]{:S(2)}, u32[]{:S(2)}) async-start(bf16[16,192,128]{2,1,0:T(8,128)(2,1)} %project.1), calls=%async_computation | async-start | bytes 1572864 | tf_op jit(solution)/shard_map/all_to_all | solution.py:227
  13.4 1.1 gather_fusion
  14.6 0.1 convert_reduce_fusion
  14.7 10.1 %all-to-all-done.got_ref = bf16[16,192,128]{2,1,0:T(8,128)(2,1)S(1)} async-done(((bf16[16,192,128]{2,1,0:T(8,128)(2,1)}), bf16[16,192,128]{2,1,0:T(8,128)(2,1)S(1)}, u32[]{:S(2)}, u32[]{:S(2)}) %all-to-all-start) | async-done | bytes 786464 | tf_op jit(solution)/shard_map/all_to_all | solution.py:227
  24.9 8.5 %attention.1 = bf16[16,128,128]{2,1,0:T(8,128)(2,1)} custom-call(s32[1]{0:T(128)} %bitcast.part_ref, f32[16,2048]{1,0:T(8,128)S(1)} %bitcast.39, bf16[16,192,128]{2,1,0:T(8,128)(2,1)S(1)} %all-to-all-done.got_ref), custom_call_target="tpu_custom_call" | custom-call | tf_op jit(solution)/shard_map/attention/pallas_call | solution.py:253
  33.3 3.6 %all-to-all-start.1 = ((bf16[16,128,128]{2,1,0:T(8,128)(2,1)}), bf16[16,128,128]{2,1,0:T(8,128)(2,1)S(1)}, u32[]{:S(2)}, u32[]{:S(2)}) async-start(bf16[16,128,128]{2,1,0:T(8,128)(2,1)} %attention.1), calls=%async_computation.1 | async-start | bytes 1048576 | tf_op jit(solution)/shard_map/all_to_all | solution.py:227
  37.0 8.9 %all-to-all-done.1.got_ref = bf16[16,128,128]{2,1,0:T(8,128)(2,1)S(1)} async-done(((bf16[16,128,128]{2,1,0:T(8,128)(2,1)}), bf16[16,128,128]{2,1,0:T(8,128)(2,1)S(1)}, u32[]{:S(2)}, u32[]{:S(2)}) %all-to-all-start.1) | async-done | bytes 524320 | tf_op jit(solution)/shard_map/all_to_all | solution.py:227
  46.0 0.8 input_grad.1
  46.8 45.1 %all_to_all.30 = bf16[32,8,640]{2,1,0:T(8,128)(2,1)S(1)} all-to-all(bf16[32,8,640]{2,1,0:T(8,128)(2,1)S(1)} %bitcast.37), channel_id=1, replica_groups=mesh['seq'=16,'table'=32] {'table'}, dimensions={0} | all-to-all | bytes 655360 | tf_op jit(solution)/shard_map/all_to_all | solution.py:227
  91.9 0.5 slab.1
  92.4 13.2 %all_to_all.31.got_ref = bf16[16,32,512]{2,1,0:T(8,128)(2,1)S(1)} all-to-all(bf16[16,32,512]{2,1,0:T(8,128)(2,1)S(1)} %bitcast.35), channel_id=1, replica_groups=mesh['seq'=16,'table'=32] {'seq'}, dimensions={0} | all-to-all | bytes 1048576 | tf_op jit(solution)/shard_map/all_to_all | solution.py:227
  105.6 0.9 row_sum.1
  106.5 3.6 %all-to-all-start.4 = ((bf16[16,32,512]{2,1,0:T(8,128)(2,1)}), bf16[16,32,512]{2,1,0:T(8,128)(2,1)S(1)}, u32[]{:S(2)}, u32[]{:S(2)}) async-start(bf16[16,32,512]{2,1,0:T(8,128)(2,1)} %row_sum.1), calls=%async_computation.4 | async-start | bytes 1048576 | tf_op jit(solution)/shard_map/all_to_all | solution.py:227
  110.1 0.1 copy.18.second_ref
  110.2 9.4 %all-to-all-done.4 = bf16[16,32,512]{2,1,0:T(8,128)(2,1)S(1)} async-done(((bf16[16,32,512]{2,1,0:T(8,128)(2,1)}), bf16[16,32,512]{2,1,0:T(8,128)(2,1)S(1)}, u32[]{:S(2)}, u32[]{:S(2)}) %all-to-all-start.4) | async-done | bytes 524320 | tf_op jit(solution)/shard_map/all_to_all | solution.py:227
  119.6 1.8 %adam.1 = (bf16[512,512]{1,0:T(8,128)(2,1)}, f32[512,512]{1,0:T(8,128)}, f32[512,1]{1,0:T(8,128)S(1)}, bf16[256,512]{1,0:T(8,128)(2,1)}) custom-call(bf16[512,512]{1,0:T(8,128)(2,1)S(1)} %bitcast.36, f32[512,512]{1,0:T(8,128)S(1)} %copy-done.2, f32[512,1]{1,0:T(8,128)S(1)} %copy.18.second_ref, bf16[512,512]{1,0:T(8,128)(2,1)S(1)} %copy-done.3, ...), custom_call_target="tpu_custom_call" | custom-call | tf_op jit(solution)/shard_map/adam/pallas_call | solution.py:305
  121.4 7.0 %all-to-all-start.5 = ((bf16[32,8,512]{2,1,0:T(8,128)(2,1)}), bf16[32,8,512]{2,1,0:T(8,128)(2,1)S(1)}, u32[]{:S(2)}, u32[]{:S(2)}) async-start(bf16[32,8,512]{2,1,0:T(8,128)(2,1)} %bitcast.13), calls=%async_computation.5 | async-start | bytes 524288 | tf_op jit(solution)/shard_map/all_to_all | solution.py:227
  128.4 0.7 reduce
  129.2 21.5 %all-to-all-done.5 = bf16[32,8,512]{2,1,0:T(8,128)(2,1)S(1)} async-done(((bf16[32,8,512]{2,1,0:T(8,128)(2,1)}), bf16[32,8,512]{2,1,0:T(8,128)(2,1)S(1)}, u32[]{:S(2)}, u32[]{:S(2)}) %all-to-all-start.5) | async-done | bytes 262176 | tf_op jit(solution)/shard_map/all_to_all | solution.py:227
  150.7 0.9 event_rows.1
  (32 shorter events, 0.4 us)
Async XLA Ops:
  0.6 1.4 copy-start
  2.0 0.9 copy-start.4
  2.9 0.9 copy-start.5
  3.9 9.2 %copy-start.10 = (s32[1,128]{1,0:T(1,128)S(1)}, s32[1,128]{1,0:T(1,128)}, u32[]{:S(2)}) copy-start(s32[1,128]{1,0:T(1,128)} %param.14) | copy-start | bytes 1540
  3.9 9.3 %copy-start.8 = (s32[16,16]{1,0:T(8,128)S(1)}, s32[16,16]{1,0:T(8,128)}, u32[]{:S(2)}) copy-start(s32[16,16]{1,0:T(8,128)} %param.13) | copy-start | bytes 3076
  5.4 8.0 %copy-start.6 = (s32[16384]{0:T(1024)S(1)}, s32[16384]{0:T(1024)}, u32[]{:S(2)}) copy-start(s32[16384]{0:T(1024)} %param.16) | copy-start | bytes 196612
  5.4 8.0 %copy-start.7 = (s32[16384]{0:T(1024)S(1)}, s32[16384]{0:T(1024)}, u32[]{:S(2)}) copy-start(s32[16384]{0:T(1024)} %param.15) | copy-start | bytes 196612
  5.4 19.5 %all-to-all-start = ((bf16[16,192,128]{2,1,0:T(8,128)(2,1)}), bf16[16,192,128]{2,1,0:T(8,128)(2,1)S(1)}, u32[]{:S(2)}, u32[]{:S(2)}) async-start(bf16[16,192,128]{2,1,0:T(8,128)(2,1)} %project.1), calls=%async_computation | async-start | bytes 1572864 | tf_op jit(solution)/shard_map/all_to_all | solution.py:227
  13.4 32.5 %copy-start.1 = (bf16[512,1536]{1,0:T(8,128)(2,1)S(1)}, bf16[512,1536]{1,0:T(8,128)(2,1)}, u32[]{:S(2)}) copy-start(bf16[512,1536]{1,0:T(8,128)(2,1)} %proj_ref.3) | copy-start | bytes 4718596
  33.3 12.7 %all-to-all-start.1 = ((bf16[16,128,128]{2,1,0:T(8,128)(2,1)}), bf16[16,128,128]{2,1,0:T(8,128)(2,1)S(1)}, u32[]{:S(2)}, u32[]{:S(2)}) async-start(bf16[16,128,128]{2,1,0:T(8,128)(2,1)} %attention.1), calls=%async_computation.1 | async-start | bytes 1048576 | tf_op jit(solution)/shard_map/all_to_all | solution.py:227
  92.4 17.7 %copy-start.9 = (f32[512]{0:T(512)S(1)}, f32[512]{0:T(512)}, u32[]{:S(2)}) copy-start(f32[512]{0:T(512)} %param.19) | copy-start | bytes 6148
  92.4 27.2 %copy-start.2 = (f32[512,512]{1,0:T(8,128)S(1)}, f32[512,512]{1,0:T(8,128)}, u32[]{:S(2)}) copy-start(f32[512,512]{1,0:T(8,128)} %moment_ref.1) | copy-start | bytes 3145732
  92.4 27.2 %copy-start.3 = (bf16[512,512]{1,0:T(8,128)(2,1)S(1)}, bf16[512,512]{1,0:T(8,128)(2,1)}, u32[]{:S(2)}) copy-start(bf16[512,512]{1,0:T(8,128)(2,1)} %table_ref.1) | copy-start | bytes 1572868
  106.5 13.1 %all-to-all-start.4 = ((bf16[16,32,512]{2,1,0:T(8,128)(2,1)}), bf16[16,32,512]{2,1,0:T(8,128)(2,1)S(1)}, u32[]{:S(2)}, u32[]{:S(2)}) async-start(bf16[16,32,512]{2,1,0:T(8,128)(2,1)} %row_sum.1), calls=%async_computation.4 | async-start | bytes 1048576 | tf_op jit(solution)/shard_map/all_to_all | solution.py:227
  121.4 29.3 %all-to-all-start.5 = ((bf16[32,8,512]{2,1,0:T(8,128)(2,1)}), bf16[32,8,512]{2,1,0:T(8,128)(2,1)S(1)}, u32[]{:S(2)}, u32[]{:S(2)}) async-start(bf16[32,8,512]{2,1,0:T(8,128)(2,1)} %bitcast.13), calls=%async_computation.5 | async-start | bytes 524288 | tf_op jit(solution)/shard_map/all_to_all | solution.py:227

commit v3 on v2

--- a/solution.py
+++ b/solution.py
@@ -1,3 +1,4 @@
+import functools
 import math
 
 import jax
@@ -37,102 +38,112 @@
     return jnp.where(low_lanes(first.shape), swap_halves(first), second)
 
 
-def project_kernel(x_ref, proj_ref, grad_ref, send_ref):
-    features = x_ref.shape[1]
-    rows = x_ref.shape[0]
+def project_kernel(shift, x_hbm, proj_hbm, grad_hbm, send_ref, x_s, proj_s, grad_s, sems):
+    rows, features = x_s.shape
+    count = send_ref.shape[0]
     half = rows // 2
-    x = x_ref[...]
-    for pair in range(HEADS // 2):
+    pairs = HEADS // 2
+    loads = [pltpu.make_async_copy(x_hbm, x_s, sems.at[pairs])]
+    loads.append(pltpu.make_async_copy(grad_hbm, grad_s, sems.at[pairs + 1]))
+    for load in loads:
+        load.start()
+    for third in range(3):
+        at = pl.ds(third * features, features)
+        loads.append(pltpu.make_async_copy(proj_hbm.at[:, at], proj_s.at[:, at], sems.at[third]))
+        loads[-1].start()
+    for load in loads:
+        load.wait()
+    x = x_s[...]
+    for pair in range(pairs):
         at = pair * LANES
-        parts = [
+        queries, keys, values = [
             jnp.dot(
-                x, proj_ref[:, third * features + at : third * features + at + LANES],
+                x, proj_s[:, third * features + at : third * features + at + LANES],
                 preferred_element_type=f32,
             )
             for third in range(3)
         ]
-        cot = grad_ref[:, at : at + LANES].astype(f32)
-        queries, keys, values = parts
+        cot = grad_s[:, at : at + LANES].astype(f32)
         for odd, join in ((0, pair_low), (1, pair_high)):
             query_grad = join(queries, cot).astype(bf16)
             key_value = join(keys, values).astype(bf16)
             for part in range(2):
-                slot = 2 * (2 * pair + odd) + part
+                slot = (2 * (2 * pair + odd) + part - shift) % count
                 send_ref[slot, 0:rows, :] = query_grad
                 send_ref[slot, rows : rows + half, :] = key_value[part * half : part * half + half]
 
 
-def attention_kernel(part_ref, seen_ref, got_ref, out_ref, key_s, value_s, total_s):
+def attention_kernel(shift, part_ref, seen_ref, got_ref, out_ref, key_s, value_s, total_s):
     blocks = got_ref.shape[0]
     rows = out_ref.shape[1]
     half = rows // 2
     tile = 2 * rows
     history_scale = 1.0 / math.sqrt(rows * blocks)
     part = part_ref[0]
-    both = got_ref[:, rows : rows + half, :].reshape(blocks * half, LANES)
-    low = low_lanes(both.shape)
-    zero = jnp.zeros_like(both)
-    key_s[...] = jnp.where(low, both * jnp.bfloat16(0.0625), zero)
-    value_s[...] = jnp.where(low, zero, both)
+    low = low_lanes((half, LANES))
+    for block in range(blocks):
+        both = got_ref[(block - shift) % blocks, rows : rows + half, :]
+        zero = jnp.zeros_like(both)
+        key_s[block * half : block * half + half, :] = jnp.where(
+            low, both * jnp.bfloat16(0.0625), zero
+        )
+        value_s[block * half : block * half + half, :] = jnp.where(low, zero, both)
     key_row = lax.broadcasted_iota(jnp.int32, (rows, tile), 0)
     query_col = lax.broadcasted_iota(jnp.int32, (rows, tile), 1)
     key_pos = (key_row // half) * rows + part * half + key_row % half
     causal = (key_pos <= query_col).astype(f32)
     for step in range(blocks // 2):
-        query_grad = got_ref[2 * step : 2 * step + 2, 0:rows, :].reshape(tile, LANES)
-        query_total = jnp.zeros((tile, LANES), f32)
-        for chunk in range(step + 1):
-            keys = key_s[chunk * rows : chunk * rows + rows, :]
-            values = value_s[chunk * rows : chunk * rows + rows, :]
-            half_scores = lax.dot_general(
-                keys, query_grad, (((1,), (1,)), ((), ())), preferred_element_type=f32
+        first = step * rows
+        count = first + rows
+        place = (2 * step - shift) % blocks
+        query_grad = got_ref[place : place + 2, 0:rows, :].reshape(tile, LANES)
+        keys = key_s[0:count, :]
+        half_scores = lax.dot_general(
+            keys, query_grad, (((1,), (1,)), ((), ())), preferred_element_type=f32
+        )
+        weight_grad = lax.dot_general(
+            value_s[0:count, :], query_grad, (((1,), (1,)), ((), ())), preferred_element_type=f32
+        )
+        seen = [
+            jnp.broadcast_to(
+                seen_ref[block : block + 1, step * tile : step * tile + tile], (half, tile)
             )
-            weight_grad = lax.dot_general(
-                values, query_grad, (((1,), (1,)), ((), ())), preferred_element_type=f32
-            )
-            seen = jnp.concatenate(
-                [
-                    jnp.broadcast_to(
-                        seen_ref[2 * chunk + b : 2 * chunk + b + 1, step * tile : step * tile + tile],
-                        (half, tile),
-                    )
-                    for b in range(2)
-                ],
-                axis=0,
-            )
-            if chunk == step:
-                seen = seen * causal
-            gate2 = (1.0 + jnp.tanh(half_scores)) * seen
-            weights = half_scores * gate2
-            score_grad = (weight_grad * (gate2 + weights * (2.0 - gate2))).astype(bf16)
-            weights = weights.astype(bf16)
-            key_part = jnp.dot(score_grad, query_grad, preferred_element_type=f32)
-            value_part = jnp.dot(weights, query_grad, preferred_element_type=f32)
-            joined = jnp.where(low_lanes(key_part.shape), key_part, value_part)
-            if chunk == step:
-                total_s[chunk * rows : chunk * rows + rows, :] = joined
-            else:
-                total_s[chunk * rows : chunk * rows + rows, :] += joined
-            query_total += lax.dot_general(
-                score_grad, keys, (((0,), (0,)), ((), ())), preferred_element_type=f32
-            )
-        query_total = query_total * history_scale
+            for block in range(2 * step + 2)
+        ]
+        for b in range(2):
+            seen[2 * step + b] = seen[2 * step + b] * causal[b * half : b * half + half]
+        gate2 = (1.0 + jnp.tanh(half_scores)) * jnp.concatenate(seen, axis=0)
+        weights = half_scores * gate2
+        score_grad = (weight_grad * (gate2 + weights * (2.0 - gate2))).astype(bf16)
+        weights = weights.astype(bf16)
+        key_part = jnp.dot(score_grad, query_grad, preferred_element_type=f32)
+        value_part = jnp.dot(weights, query_grad, preferred_element_type=f32)
+        joined = jnp.where(low_lanes(key_part.shape), key_part, value_part)
+        if step > 0:
+            total_s[0:first, :] += joined[0:first]
+        total_s[first:count, :] = joined[first:count]
+        query_total = history_scale * lax.dot_general(
+            score_grad, keys, (((0,), (0,)), ((), ())), preferred_element_type=f32
+        )
         for b in range(2):
             top = query_total[b * rows : b * rows + half]
             bottom = query_total[b * rows + half : b * rows + rows]
-            out_ref[2 * step + b, half:rows, :] = (top + swap_halves(bottom)).astype(bf16)
+            out_ref[place + b, half:rows, :] = (top + swap_halves(bottom)).astype(bf16)
     scale = jnp.where(low_lanes((1, LANES)), history_scale * 0.0625, history_scale)
-    out_ref[:, 0:half, :] = (total_s[...] * scale).astype(bf16).reshape(blocks, half, LANES)
-
-
-def input_grad_kernel(got_ref, proj_ref, target_ref, digits_ref, send_ref):
-    rows = got_ref.shape[1]
+    for block in range(blocks):
+        out_ref[(block - shift) % blocks, 0:half, :] = (
+            total_s[block * half : block * half + half, :] * scale
+        ).astype(bf16)
+
+
+def input_grad_kernel(shift, got_ref, proj_ref, target_ref, digits_ref, send_ref):
+    count, rows = got_ref.shape[0:2]
     half = rows // 2
     queries, keys, values = [], [], []
     for pair in range(HEADS // 2):
         query, joint = [], []
         for odd in range(2):
-            slot = 2 * (2 * pair + odd)
+            slot = (2 * (2 * pair + odd) - shift) % count
             query.append(
                 got_ref[slot, half:rows, :].astype(f32) + got_ref[slot + 1, half:rows, :].astype(f32)
             )
@@ -223,8 +234,12 @@
     return jax.ShapeDtypeStruct(dims, kind)
 
 
-def exchange(array, axis):
-    return lax.all_to_all(array, axis, split_axis=0, concat_axis=0, tiled=True)
+def exchange(array, axis, shift):
+    count = array.shape[0]
+    order = [[(member + shift) % count for member in range(count)]]
+    return lax.all_to_all(
+        array, axis, split_axis=0, concat_axis=0, axis_index_groups=order, tiled=True
+    )
 
 
 def body(events_x, proj, out_grad, block_mask, item_ids, owner_of, local_of, table, moment, second):
@@ -237,21 +252,30 @@
     capacity = 2 * tokens // owner_count
     slots = owner_count * capacity
     half = tokens // 2
-
+    seq_shift = seq_count // 2 + math.isqrt(seq_count) // 2
+    table_shift = owner_count // 2
+
+    in_hbm = pl.BlockSpec(memory_space=pltpu.MemorySpace.HBM)
     send = pl.pallas_call(
-        project_kernel,
+        functools.partial(project_kernel, seq_shift),
         out_shape=shape((seq_count, tokens + half, LANES), bf16),
-        compiler_params=limit(8), name="project",
+        in_specs=[in_hbm, in_hbm, in_hbm],
+        scratch_shapes=[
+            pltpu.VMEM((tokens, features), bf16),
+            pltpu.VMEM((features, 3 * features), bf16),
+            pltpu.VMEM((tokens, features), bf16),
+            pltpu.SemaphoreType.DMA((HEADS // 2 + 2,)),
+        ],
+        compiler_params=limit(60), name="project",
     )(events_x[0], proj, out_grad[0])
-    got = exchange(send, "seq")
+    got = exchange(send, "seq", seq_shift)
 
     block_ids = jnp.arange(seq_count)
-    query_blk = jnp.arange(seq_count * tokens) // tokens
     visible = (block_mask == 1) | (block_ids[:, None] == block_ids[None, :])
     seen = jnp.repeat(visible.T.astype(f32), tokens, axis=1)
     part = (position % 2).astype(jnp.int32).reshape(1)
     back = pl.pallas_call(
-        attention_kernel,
+        functools.partial(attention_kernel, seq_shift),
         out_shape=shape((seq_count, tokens, LANES), bf16),
         in_specs=[
             pl.BlockSpec(memory_space=pltpu.SMEM),
@@ -263,9 +287,9 @@
             pltpu.VMEM((seq_count * half, LANES), bf16),
             pltpu.VMEM((seq_count * half, LANES), f32),
         ],
-        compiler_params=limit(16), name="attention",
+        compiler_params=limit(24), name="attention",
     )(part, seen, got)
-    got_back = exchange(back, "seq")
+    got_back = exchange(back, "seq", seq_shift)
 
     place_of = owner_of * slab_rows + local_of
     place = place_of[item_ids[0]]
@@ -274,7 +298,8 @@
     event = jnp.arange(tokens)
     earlier = (owners[:, None] == owners[None, :]) & (event[:, None] < event[None, :])
     rank = jnp.sum(earlier.astype(jnp.int32), axis=0)
-    target = (owners * capacity + rank)[None, :]
+    member = (owners - table_shift) % owner_count
+    target = (member * capacity + rank)[None, :]
     lane = jnp.arange(LANES)[None, :]
     digits = jnp.where(
         lane == 0,
@@ -282,25 +307,25 @@
         jnp.where(lane == 1, (slab_index % DIGIT)[:, None], 0),
     ).astype(bf16)
     send_rows = pl.pallas_call(
-        input_grad_kernel,
+        functools.partial(input_grad_kernel, seq_shift),
         out_shape=shape((slots, features + LANES), bf16),
         compiler_params=limit(12), name="input_grad",
     )(got_back, proj, target, digits)
     got_rows = exchange(
-        send_rows.reshape(owner_count, capacity, features + LANES), "table"
+        send_rows.reshape(owner_count, capacity, features + LANES), "table", table_shift
     ).reshape(slots, features + LANES)
 
     slab = pl.pallas_call(slab_kernel, out_shape=shape((slab_rows, features), bf16), compiler_params=limit(8), name="slab")(
         got_rows
     )
     share = slab_rows // seq_count
-    parts = exchange(slab.reshape(seq_count, share, features), "seq")
+    parts = exchange(slab.reshape(seq_count, share, features), "seq", seq_shift)
     copies = pl.pallas_call(
         sum_kernel,
         out_shape=shape((seq_count, share, features), bf16),
         compiler_params=limit(8), name="row_sum",
     )(parts)
-    item_grad = exchange(copies, "seq").reshape(slab_rows, features)
+    item_grad = exchange(copies, "seq", seq_shift).reshape(slab_rows, features)
 
     new_table, new_moment, new_second, reply = pl.pallas_call(
         adam_kernel,
@@ -326,7 +351,7 @@
         ),
         compiler_params=limit(12), name="adam",
     )(item_grad, moment, second[:, None], table, got_rows)
-    returned = exchange(reply.reshape(owner_count, capacity, features), "table")
+    returned = exchange(reply.reshape(owner_count, capacity, features), "table", table_shift)
     event_rows = pl.pallas_call(
         event_kernel,
         out_shape=shape((tokens, features), bf16),

time: 152 us -> 136 us (0.89)
  waiting for transfers between devices: 50 us -> 26.7 us
  starting transfers between devices: 21.9 us -> 37.9 us
  blocking collectives: 58.2 us -> 54.8 us
  local copies, waits for them, and re-layouts: 4.75 us -> 1.55 us
  Pallas kernels: 14.8 us -> 12.7 us
    all_to_all x4, waiting for transfers between devices: 50 us -> 26.7 us  [exchange(): lax.all_to_all(array, axis, split_axis=0, concat_axis=0, axis_index_group...]
    all_to_all x4, starting transfers between devices: 21.9 us -> 37.9 us  [exchange(): lax.all_to_all(array, axis, split_axis=0, concat_axis=0, axis_index_group...]
    all_to_all x2, blocking collectives: 58.2 us -> 54.8 us  [exchange(): lax.all_to_all(array, axis, split_axis=0, concat_axis=0, axis_index_group...]
    unnamed x23 -> x17, local copies, waits for them, and re-layouts: 3.3 us -> 0.09 us
    pallas_call x3, Pallas kernels: 10.8 us -> 8.63 us  [the longest x1 4.7 us: body(): pl.pallas_call(functools.partial(attention_kernel, seq_shift), out_shape=...]
where the time goes in v3:
time: 136 us; the launch traced here: 135 us
  blocking collectives  54.8 us (40%)
  starting transfers between devices  37.9 us (28%)
  waiting for transfers between devices  26.7 us (20%)
  Pallas kernels  12.7 us (9%)
  local copies, waits for them, and re-layouts  1.55 us (1%)
    all_to_all x2, blocking collectives, exchange(): lax.all_to_all(array, axis, split_axis=0, concat_axis=0, axis_index_group...  54.8 us
    all_to_all x4, starting transfers between devices, exchange(): lax.all_to_all(array, axis, split_axis=0, concat_axis=0, axis_index_group...  37.9 us
    all_to_all x4, waiting for transfers between devices, exchange(): lax.all_to_all(array, axis, split_axis=0, concat_axis=0, axis_index_group...  26.7 us
    pallas_call x1, Pallas kernels, body(): pl.pallas_call(functools.partial(attention_kernel, seq_shift), out_shape=...  4.7 us
    pallas_call x1, Pallas kernels, body(): pl.pallas_call(functools.partial(project_kernel, seq_shift), out_shape=sh...  3.08 us
  transfers between devices with their start and end apart: 4, of which 4 were waited for; matrix products, arithmetic and copies ran while one was open for 2% of the time, Pallas kernels for 0%

profile of v3, /device:TPU:1, one launch (start us, length us, event | category | flops | bytes accessed | tf_op | source)
XLA Modules:
  0.0 135.5 jit_solution(9530251805606890324)
XLA Ops:
  0.7 3.1 %project.1 = bf16[16,192,128]{2,1,0:T(8,128)(2,1)} custom-call(bf16[128,512]{1,0:T(8,128)(2,1)} %bitcast.41, bf16[512,1536]{1,0:T(8,128)(2,1)} %proj_ref.1, bf16[128,512]{1,0:T(8,128)(2,1)} %bitcast.42), custom_call_target="tpu_custom_call" | custom-call | tf_op jit(solution)/shard_map/project/pallas_call | solution.py:259
  3.8 9.8 %all-to-all-start = ((bf16[16,192,128]{2,1,0:T(8,128)(2,1)}), bf16[16,192,128]{2,1,0:T(8,128)(2,1)S(1)}, u32[]{:S(2)}, u32[]{:S(2)}) async-start(bf16[16,192,128]{2,1,0:T(8,128)(2,1)} %project.1), calls=%async_computation | async-start | bytes 1572864 | tf_op jit(solution)/shard_map/all_to_all | solution.py:240
  13.6 0.1 copy.17
  13.7 0.1 broadcast_in_dim.56
  13.9 1.1 gather_fusion
  15.1 0.1 convert_reduce_fusion
  15.2 4.4 %all-to-all-done.got_ref = bf16[16,192,128]{2,1,0:T(8,128)(2,1)S(1)} async-done(((bf16[16,192,128]{2,1,0:T(8,128)(2,1)}), bf16[16,192,128]{2,1,0:T(8,128)(2,1)S(1)}, u32[]{:S(2)}, u32[]{:S(2)}) %all-to-all-start) | async-done | bytes 786464 | tf_op jit(solution)/shard_map/all_to_all | solution.py:240
  19.5 4.7 %attention.1 = bf16[16,128,128]{2,1,0:T(8,128)(2,1)} custom-call(s32[1]{0:T(128)} %bitcast.part_ref, f32[16,2048]{1,0:T(8,128)S(1)} %bitcast.39, bf16[16,192,128]{2,1,0:T(8,128)(2,1)S(1)} %all-to-all-done.got_ref), custom_call_target="tpu_custom_call" | custom-call | tf_op jit(solution)/shard_map/attention/pallas_call | solution.py:277
  24.2 7.0 %all-to-all-start.1 = ((bf16[16,128,128]{2,1,0:T(8,128)(2,1)}), bf16[16,128,128]{2,1,0:T(8,128)(2,1)S(1)}, u32[]{:S(2)}, u32[]{:S(2)}) async-start(bf16[16,128,128]{2,1,0:T(8,128)(2,1)} %attention.1), calls=%async_computation.1 | async-start | bytes 1048576 | tf_op jit(solution)/shard_map/all_to_all | solution.py:240
  31.2 0.1 select_convert_fusion.digits_ref
  31.3 4.1 %all-to-all-done.1.got_ref = bf16[16,128,128]{2,1,0:T(8,128)(2,1)S(1)} async-done(((bf16[16,128,128]{2,1,0:T(8,128)(2,1)}), bf16[16,128,128]{2,1,0:T(8,128)(2,1)S(1)}, u32[]{:S(2)}, u32[]{:S(2)}) %all-to-all-start.1) | async-done | bytes 524320 | tf_op jit(solution)/shard_map/all_to_all | solution.py:240
  35.4 0.9 input_grad.1
  36.3 41.0 %all_to_all.30 = bf16[32,8,640]{2,1,0:T(8,128)(2,1)S(1)} all-to-all(bf16[32,8,640]{2,1,0:T(8,128)(2,1)S(1)} %bitcast.37), channel_id=1, replica_groups={{16,17,18,19,20,21,22,23,24,25,26,27,28,29,30,31,0,1,2,3,4,5,6,7,8,9,10..., dimensions={0} | all-to-all | bytes 655360 | tf_op jit(solution)/shard_map/all_to_all | solution.py:240
  77.3 0.5 slab.1
  77.8 13.8 %all_to_all.31.got_ref = bf16[16,32,512]{2,1,0:T(8,128)(2,1)S(1)} all-to-all(bf16[16,32,512]{2,1,0:T(8,128)(2,1)S(1)} %bitcast.35), channel_id=1, replica_groups={{320,352,384,416,448,480,0,32,64,96,128,160,192,224,256,288},{321,353,3..., dimensions={0} | all-to-all | bytes 1048576 | tf_op jit(solution)/shard_map/all_to_all | solution.py:240
  91.6 0.9 row_sum.1
  92.5 7.1 %all-to-all-start.4 = ((bf16[16,32,512]{2,1,0:T(8,128)(2,1)}), bf16[16,32,512]{2,1,0:T(8,128)(2,1)S(1)}, u32[]{:S(2)}, u32[]{:S(2)}) async-start(bf16[16,32,512]{2,1,0:T(8,128)(2,1)} %row_sum.1), calls=%async_computation.4 | async-start | bytes 1048576 | tf_op jit(solution)/shard_map/all_to_all | solution.py:240
  99.5 0.1 copy.18.second_ref
  99.7 6.4 %all-to-all-done.4 = bf16[16,32,512]{2,1,0:T(8,128)(2,1)S(1)} async-done(((bf16[16,32,512]{2,1,0:T(8,128)(2,1)}), bf16[16,32,512]{2,1,0:T(8,128)(2,1)S(1)}, u32[]{:S(2)}, u32[]{:S(2)}) %all-to-all-start.4) | async-done | bytes 524320 | tf_op jit(solution)/shard_map/all_to_all | solution.py:240
  106.1 1.8 %adam.1 = (bf16[512,512]{1,0:T(8,128)(2,1)}, f32[512,512]{1,0:T(8,128)}, f32[512,1]{1,0:T(8,128)S(1)}, bf16[256,512]{1,0:T(8,128)(2,1)}) custom-call(bf16[512,512]{1,0:T(8,128)(2,1)S(1)} %bitcast.36, f32[512,512]{1,0:T(8,128)S(1)} %copy-done.1, f32[512,1]{1,0:T(8,128)S(1)} %copy.18.second_ref, bf16[512,512]{1,0:T(8,128)(2,1)S(1)} %copy-done.2, ...), custom_call_target="tpu_custom_call" | custom-call | tf_op jit(solution)/shard_map/adam/pallas_call | solution.py:330
  107.9 14.1 %all-to-all-start.5 = ((bf16[32,8,512]{2,1,0:T(8,128)(2,1)}), bf16[32,8,512]{2,1,0:T(8,128)(2,1)S(1)}, u32[]{:S(2)}, u32[]{:S(2)}) async-start(bf16[32,8,512]{2,1,0:T(8,128)(2,1)} %bitcast.13), calls=%async_computation.5 | async-start | bytes 524288 | tf_op jit(solution)/shard_map/all_to_all | solution.py:240
  122.0 0.7 reduce
  122.8 11.8 %all-to-all-done.5 = bf16[32,8,512]{2,1,0:T(8,128)(2,1)S(1)} async-done(((bf16[32,8,512]{2,1,0:T(8,128)(2,1)}), bf16[32,8,512]{2,1,0:T(8,128)(2,1)S(1)}, u32[]{:S(2)}, u32[]{:S(2)}) %all-to-all-start.5) | async-done | bytes 262176 | tf_op jit(solution)/shard_map/all_to_all | solution.py:240
  134.6 0.9 event_rows.1
  (26 shorter events, 0.2 us)
Async XLA Ops:
  0.6 12.9 %copy-start.7 = (s32[1,128]{1,0:T(1,128)S(1)}, s32[1,128]{1,0:T(1,128)}, u32[]{:S(2)}) copy-start(s32[1,128]{1,0:T(1,128)} %param.14) | copy-start | bytes 1540
  0.6 12.9 %copy-start.5 = (s32[16,16]{1,0:T(8,128)S(1)}, s32[16,16]{1,0:T(8,128)}, u32[]{:S(2)}) copy-start(s32[16,16]{1,0:T(8,128)} %param.13) | copy-start | bytes 3076
  3.7 10.1 %copy-start.3 = (s32[16384]{0:T(1024)S(1)}, s32[16384]{0:T(1024)}, u32[]{:S(2)}) copy-start(s32[16384]{0:T(1024)} %param.16) | copy-start | bytes 196612
  3.7 10.1 %copy-start.4 = (s32[16384]{0:T(1024)S(1)}, s32[16384]{0:T(1024)}, u32[]{:S(2)}) copy-start(s32[16384]{0:T(1024)} %param.15) | copy-start | bytes 196612
  3.8 15.8 %all-to-all-start = ((bf16[16,192,128]{2,1,0:T(8,128)(2,1)}), bf16[16,192,128]{2,1,0:T(8,128)(2,1)S(1)}, u32[]{:S(2)}, u32[]{:S(2)}) async-start(bf16[16,192,128]{2,1,0:T(8,128)(2,1)} %project.1), calls=%async_computation | async-start | bytes 1572864 | tf_op jit(solution)/shard_map/all_to_all | solution.py:240
  13.9 21.6 %copy-start = (bf16[512,1536]{1,0:T(8,128)(2,1)S(1)}, bf16[512,1536]{1,0:T(8,128)(2,1)}, u32[]{:S(2)}) copy-start(bf16[512,1536]{1,0:T(8,128)(2,1)} %proj_ref.1) | copy-start | bytes 4718596
  24.2 11.2 %all-to-all-start.1 = ((bf16[16,128,128]{2,1,0:T(8,128)(2,1)}), bf16[16,128,128]{2,1,0:T(8,128)(2,1)S(1)}, u32[]{:S(2)}, u32[]{:S(2)}) async-start(bf16[16,128,128]{2,1,0:T(8,128)(2,1)} %attention.1), calls=%async_computation.1 | async-start | bytes 1048576 | tf_op jit(solution)/shard_map/all_to_all | solution.py:240
  77.8 21.8 %copy-start.6 = (f32[512]{0:T(512)S(1)}, f32[512]{0:T(512)}, u32[]{:S(2)}) copy-start(f32[512]{0:T(512)} %param.19) | copy-start | bytes 6148
  77.8 28.3 %copy-start.1 = (f32[512,512]{1,0:T(8,128)S(1)}, f32[512,512]{1,0:T(8,128)}, u32[]{:S(2)}) copy-start(f32[512,512]{1,0:T(8,128)} %moment_ref.1) | copy-start | bytes 3145732
  77.8 28.3 %copy-start.2 = (bf16[512,512]{1,0:T(8,128)(2,1)S(1)}, bf16[512,512]{1,0:T(8,128)(2,1)}, u32[]{:S(2)}) copy-start(bf16[512,512]{1,0:T(8,128)(2,1)} %table_ref.1) | copy-start | bytes 1572868
  92.5 13.6 %all-to-all-start.4 = ((bf16[16,32,512]{2,1,0:T(8,128)(2,1)}), bf16[16,32,512]{2,1,0:T(8,128)(2,1)S(1)}, u32[]{:S(2)}, u32[]{:S(2)}) async-start(bf16[16,32,512]{2,1,0:T(8,128)(2,1)} %row_sum.1), calls=%async_computation.4 | async-start | bytes 1048576 | tf_op jit(solution)/shard_map/all_to_all | solution.py:240
  107.9 26.7 %all-to-all-start.5 = ((bf16[32,8,512]{2,1,0:T(8,128)(2,1)}), bf16[32,8,512]{2,1,0:T(8,128)(2,1)S(1)}, u32[]{:S(2)}, u32[]{:S(2)}) async-start(bf16[32,8,512]{2,1,0:T(8,128)(2,1)} %bitcast.13), calls=%async_computation.5 | async-start | bytes 524288 | tf_op jit(solution)/shard_map/all_to_all | solution.py:240

commit v4 on v3

--- a/solution.py
+++ b/solution.py
@@ -38,32 +38,23 @@
     return jnp.where(low_lanes(first.shape), swap_halves(first), second)
 
 
-def project_kernel(shift, x_hbm, proj_hbm, grad_hbm, send_ref, x_s, proj_s, grad_s, sems):
-    rows, features = x_s.shape
+def project_kernel(shift, x_ref, proj_ref, grad_ref, send_ref):
+    features = x_ref.shape[1]
+    rows = x_ref.shape[0]
+    half = rows // 2
     count = send_ref.shape[0]
-    half = rows // 2
-    pairs = HEADS // 2
-    loads = [pltpu.make_async_copy(x_hbm, x_s, sems.at[pairs])]
-    loads.append(pltpu.make_async_copy(grad_hbm, grad_s, sems.at[pairs + 1]))
-    for load in loads:
-        load.start()
-    for third in range(3):
-        at = pl.ds(third * features, features)
-        loads.append(pltpu.make_async_copy(proj_hbm.at[:, at], proj_s.at[:, at], sems.at[third]))
-        loads[-1].start()
-    for load in loads:
-        load.wait()
-    x = x_s[...]
-    for pair in range(pairs):
+    x = x_ref[...]
+    for pair in range(HEADS // 2):
         at = pair * LANES
-        queries, keys, values = [
+        parts = [
             jnp.dot(
-                x, proj_s[:, third * features + at : third * features + at + LANES],
+                x, proj_ref[:, third * features + at : third * features + at + LANES],
                 preferred_element_type=f32,
             )
             for third in range(3)
         ]
-        cot = grad_s[:, at : at + LANES].astype(f32)
+        cot = grad_ref[:, at : at + LANES].astype(f32)
+        queries, keys, values = parts
         for odd, join in ((0, pair_low), (1, pair_high)):
             query_grad = join(queries, cot).astype(bf16)
             key_value = join(keys, values).astype(bf16)
@@ -73,7 +64,7 @@
                 send_ref[slot, rows : rows + half, :] = key_value[part * half : part * half + half]
 
 
-def attention_kernel(shift, part_ref, seen_ref, got_ref, out_ref, key_s, value_s, total_s):
+def attention_kernel(shift, part_ref, seen_ref, got_ref, out_ref, key_s, value_s, total_s, key_t):
     blocks = got_ref.shape[0]
     rows = out_ref.shape[1]
     half = rows // 2
@@ -88,6 +79,7 @@
             low, both * jnp.bfloat16(0.0625), zero
         )
         value_s[block * half : block * half + half, :] = jnp.where(low, zero, both)
+    key_t[...] = key_s[...].astype(f32).T[0:half].astype(bf16)
     key_row = lax.broadcasted_iota(jnp.int32, (rows, tile), 0)
     query_col = lax.broadcasted_iota(jnp.int32, (rows, tile), 1)
     key_pos = (key_row // half) * rows + part * half + key_row % half
@@ -122,13 +114,15 @@
         if step > 0:
             total_s[0:first, :] += joined[0:first]
         total_s[first:count, :] = joined[first:count]
-        query_total = history_scale * lax.dot_general(
-            score_grad, keys, (((0,), (0,)), ((), ())), preferred_element_type=f32
+        query_total = history_scale * jnp.dot(
+            key_t[:, 0:count], score_grad, preferred_element_type=f32
         )
         for b in range(2):
-            top = query_total[b * rows : b * rows + half]
-            bottom = query_total[b * rows + half : b * rows + rows]
-            out_ref[place + b, half:rows, :] = (top + swap_halves(bottom)).astype(bf16)
+            top = query_total[:, b * rows : b * rows + half]
+            bottom = query_total[:, b * rows + half : b * rows + rows]
+            out_ref[place + b, half:rows, :] = (
+                jnp.concatenate([top, bottom], axis=0).T.astype(bf16)
+            )
     scale = jnp.where(low_lanes((1, LANES)), history_scale * 0.0625, history_scale)
     for block in range(blocks):
         out_ref[(block - shift) % blocks, 0:half, :] = (
@@ -194,18 +188,15 @@
 
 
 def adam_kernel(
-    grad_ref, moment_ref, second_ref, table_ref, digits_ref,
-    new_table_ref, new_moment_ref, new_second_ref, reply_ref,
+    grad_ref, moment_ref, second_ref, table_ref, digits_ref, new_table_ref, new_second_ref, reply_ref
 ):
     item_grad = grad_ref[...].astype(f32)
-    new_moment = first_decay * moment_ref[...] + (1.0 - first_decay) * item_grad
-    new_moment_ref[...] = new_moment
     mean = jnp.mean(item_grad * item_grad, axis=1, keepdims=True)
     new_second = second_decay * second_ref[...] + (1.0 - second_decay) * mean
     new_second_ref[...] = new_second
-    new_table = (
-        table_ref[...].astype(f32) - step_rate * new_moment / (jnp.sqrt(new_second) + epsilon)
-    ).astype(bf16)
+    rate = step_rate / (jnp.sqrt(new_second) + epsilon)
+    new_moment = first_decay * moment_ref[...] + (1.0 - first_decay) * item_grad
+    new_table = (table_ref[...].astype(f32) - new_moment * rate).astype(bf16)
     new_table_ref[...] = new_table
     select = slot_rows(digits_ref[...], new_table.shape[0])
     reply_ref[...] = jnp.dot(select, new_table, preferred_element_type=f32).astype(bf16)
@@ -253,19 +244,11 @@
     slots = owner_count * capacity
     half = tokens // 2
     seq_shift = seq_count // 2 + math.isqrt(seq_count) // 2
-    table_shift = owner_count // 2
-
-    in_hbm = pl.BlockSpec(memory_space=pltpu.MemorySpace.HBM)
+    table_shift = owner_count // 2 + 2
+
     send = pl.pallas_call(
         functools.partial(project_kernel, seq_shift),
         out_shape=shape((seq_count, tokens + half, LANES), bf16),
-        in_specs=[in_hbm, in_hbm, in_hbm],
-        scratch_shapes=[
-            pltpu.VMEM((tokens, features), bf16),
-            pltpu.VMEM((features, 3 * features), bf16),
-            pltpu.VMEM((tokens, features), bf16),
-            pltpu.SemaphoreType.DMA((HEADS // 2 + 2,)),
-        ],
         compiler_params=limit(60), name="project",
     )(events_x[0], proj, out_grad[0])
     got = exchange(send, "seq", seq_shift)
@@ -286,6 +269,7 @@
             pltpu.VMEM((seq_count * half, LANES), bf16),
             pltpu.VMEM((seq_count * half, LANES), bf16),
             pltpu.VMEM((seq_count * half, LANES), f32),
+            pltpu.VMEM((half, seq_count * half), bf16),
         ],
         compiler_params=limit(24), name="attention",
     )(part, seen, got)
@@ -327,11 +311,10 @@
     )(parts)
     item_grad = exchange(copies, "seq", seq_shift).reshape(slab_rows, features)
 
-    new_table, new_moment, new_second, reply = pl.pallas_call(
+    new_table, new_second, reply = pl.pallas_call(
         adam_kernel,
         out_shape=(
             shape((slab_rows, features), bf16),
-            shape((slab_rows, features), f32),
             shape((slab_rows, 1), f32),
             shape((slots, features), bf16),
         ),
@@ -345,12 +328,12 @@
         ],
         out_specs=(
             whole((slab_rows, features)),
-            whole((slab_rows, features)),
             whole((slab_rows, 1)),
             whole((slots, features)),
         ),
         compiler_params=limit(12), name="adam",
     )(item_grad, moment, second[:, None], table, got_rows)
+    new_moment = first_decay * moment + (1.0 - first_decay) * item_grad.astype(f32)
     returned = exchange(reply.reshape(owner_count, capacity, features), "table", table_shift)
     event_rows = pl.pallas_call(
         event_kernel,

time: 136 us -> 134 us (0.985)
  starting transfers between devices: 37.9 us -> 36 us
    all_to_all x4, starting transfers between devices: 37.9 us -> 36 us  [exchange(): lax.all_to_all(array, axis, split_axis=0, concat_axis=0, axis_index_group...]
  transfers between devices with their start and end apart: 4 -> 4, of which waited for: 4 -> 4; matrix products, arithmetic and copies ran while one was open for 2% -> 3% of each run, Pallas kernels for 0% -> 0%
where the time goes in v4:
time: 134 us; the launch traced here: 133 us
  blocking collectives  54.7 us (41%)
  starting transfers between devices  36 us (27%)
  waiting for transfers between devices  26.3 us (20%)
  Pallas kernels  11.9 us (9%)
  other arithmetic  2.21 us (2%)
  local copies, waits for them, and re-layouts  1.54 us (1%)
    all_to_all x2, blocking collectives, exchange(): lax.all_to_all(array, axis, split_axis=0, concat_axis=0, axis_index_group...  54.7 us
    all_to_all x4, starting transfers between devices, exchange(): lax.all_to_all(array, axis, split_axis=0, concat_axis=0, axis_index_group...  36 us
    all_to_all x4, waiting for transfers between devices, exchange(): lax.all_to_all(array, axis, split_axis=0, concat_axis=0, axis_index_group...  26.3 us
    pallas_call x1, Pallas kernels, body(): pl.pallas_call(functools.partial(attention_kernel, seq_shift), out_shape=...  4.35 us
    pallas_call x1, Pallas kernels, body(): pl.pallas_call(functools.partial(project_kernel, seq_shift), out_shape=sh...  2.94 us
  transfers between devices with their start and end apart: 4, of which 4 were waited for; matrix products, arithmetic and copies ran while one was open for 3% of the time, Pallas kernels for 0%

profile of v4, /device:TPU:1, one launch (start us, length us, event | category | flops | bytes accessed | tf_op | source)
XLA Modules:
  0.0 133.5 jit_solution(15618315128998433934)
XLA Ops:
  0.7 2.9 %project.1 = bf16[16,192,128]{2,1,0:T(8,128)(2,1)} custom-call(bf16[128,512]{1,0:T(8,128)(2,1)} %bitcast.42, bf16[512,1536]{1,0:T(8,128)(2,1)} %proj_ref.3, bf16[128,512]{1,0:T(8,128)(2,1)} %bitcast.43), custom_call_target="tpu_custom_call" | custom-call | tf_op jit(solution)/shard_map/project/pallas_call | solution.py:249
  3.6 9.8 %all-to-all-start = ((bf16[16,192,128]{2,1,0:T(8,128)(2,1)}), bf16[16,192,128]{2,1,0:T(8,128)(2,1)S(1)}, u32[]{:S(2)}, u32[]{:S(2)}) async-start(bf16[16,192,128]{2,1,0:T(8,128)(2,1)} %project.1), calls=%async_computation | async-start | bytes 1572864 | tf_op jit(solution)/shard_map/all_to_all | solution.py:231
  13.5 0.1 broadcast_in_dim.56
  13.7 1.1 gather_fusion
  14.9 0.1 convert_reduce_fusion
  15.0 4.4 %all-to-all-done.got_ref = bf16[16,192,128]{2,1,0:T(8,128)(2,1)S(1)} async-done(((bf16[16,192,128]{2,1,0:T(8,128)(2,1)}), bf16[16,192,128]{2,1,0:T(8,128)(2,1)S(1)}, u32[]{:S(2)}, u32[]{:S(2)}) %all-to-all-start) | async-done | bytes 786464 | tf_op jit(solution)/shard_map/all_to_all | solution.py:231
  19.4 4.3 %attention.1 = bf16[16,128,128]{2,1,0:T(8,128)(2,1)} custom-call(s32[1]{0:T(128)} %bitcast.part_ref, f32[16,2048]{1,0:T(8,128)S(1)} %bitcast.40, bf16[16,192,128]{2,1,0:T(8,128)(2,1)S(1)} %all-to-all-done.got_ref), custom_call_target="tpu_custom_call" | custom-call | tf_op jit(solution)/shard_map/attention/pallas_call | solution.py:260
  23.7 7.0 %all-to-all-start.1 = ((bf16[16,128,128]{2,1,0:T(8,128)(2,1)}), bf16[16,128,128]{2,1,0:T(8,128)(2,1)S(1)}, u32[]{:S(2)}, u32[]{:S(2)}) async-start(bf16[16,128,128]{2,1,0:T(8,128)(2,1)} %attention.1), calls=%async_computation.1 | async-start | bytes 1048576 | tf_op jit(solution)/shard_map/all_to_all | solution.py:231
  30.7 0.1 select_convert_fusion.digits_ref
  30.8 4.1 %all-to-all-done.1.got_ref = bf16[16,128,128]{2,1,0:T(8,128)(2,1)S(1)} async-done(((bf16[16,128,128]{2,1,0:T(8,128)(2,1)}), bf16[16,128,128]{2,1,0:T(8,128)(2,1)S(1)}, u32[]{:S(2)}, u32[]{:S(2)}) %all-to-all-start.1) | async-done | bytes 524320 | tf_op jit(solution)/shard_map/all_to_all | solution.py:231
  34.9 0.9 input_grad.1
  35.8 40.8 %all_to_all.30 = bf16[32,8,640]{2,1,0:T(8,128)(2,1)S(1)} all-to-all(bf16[32,8,640]{2,1,0:T(8,128)(2,1)S(1)} %bitcast.38), channel_id=1, replica_groups={{18,19,20,21,22,23,24,25,26,27,28,29,30,31,0,1,2,3,4,5,6,7,8,9,10,11,12..., dimensions={0} | all-to-all | bytes 655360 | tf_op jit(solution)/shard_map/all_to_all | solution.py:231
  76.6 0.5 slab.1
  77.1 13.8 %all_to_all.31.got_ref = bf16[16,32,512]{2,1,0:T(8,128)(2,1)S(1)} all-to-all(bf16[16,32,512]{2,1,0:T(8,128)(2,1)S(1)} %bitcast.37), channel_id=1, replica_groups={{320,352,384,416,448,480,0,32,64,96,128,160,192,224,256,288},{321,353,3..., dimensions={0} | all-to-all | bytes 1048576 | tf_op jit(solution)/shard_map/all_to_all | solution.py:231
  91.0 0.9 row_sum.1
  91.9 7.3 %all-to-all-start.4 = ((bf16[16,32,512]{2,1,0:T(8,128)(2,1)}), bf16[16,32,512]{2,1,0:T(8,128)(2,1)S(1)}, u32[]{:S(2)}, u32[]{:S(2)}) async-start(bf16[16,32,512]{2,1,0:T(8,128)(2,1)} %row_sum.1), calls=%async_computation.4 | async-start | bytes 1048576 | tf_op jit(solution)/shard_map/all_to_all | solution.py:231
  99.2 0.1 copy.18.second_ref
  99.3 6.7 %all-to-all-done.4 = bf16[16,32,512]{2,1,0:T(8,128)(2,1)S(1)} async-done(((bf16[16,32,512]{2,1,0:T(8,128)(2,1)}), bf16[16,32,512]{2,1,0:T(8,128)(2,1)S(1)}, u32[]{:S(2)}, u32[]{:S(2)}) %all-to-all-start.4) | async-done | bytes 524320 | tf_op jit(solution)/shard_map/all_to_all | solution.py:231
  106.0 1.5 %adam.1 = (bf16[512,512]{1,0:T(8,128)(2,1)}, f32[512,1]{1,0:T(8,128)S(1)}, bf16[256,512]{1,0:T(8,128)(2,1)}) custom-call(bf16[512,512]{1,0:T(8,128)(2,1)S(1)} %bitcast.34, f32[512,512]{1,0:T(8,128)S(1)} %copy-done.1, f32[512,1]{1,0:T(8,128)S(1)} %copy.18.second_ref, bf16[512,512]{1,0:T(8,128)(2,1)S(1)} %copy-done.2, bf16[256,640]{1,0:T(8,128)(2,1)S(1)} %bitcast.36), custom_call_target="tpu_custom_call" | custom-call | tf_op jit(solution)/shard_map/adam/pallas_call | solution.py:314
  107.5 12.0 %all-to-all-start.5 = ((bf16[32,8,512]{2,1,0:T(8,128)(2,1)}), bf16[32,8,512]{2,1,0:T(8,128)(2,1)S(1)}, u32[]{:S(2)}, u32[]{:S(2)}) async-start(bf16[32,8,512]{2,1,0:T(8,128)(2,1)} %bitcast.13), calls=%async_computation.5 | async-start | bytes 524288 | tf_op jit(solution)/shard_map/all_to_all | solution.py:231
  119.5 0.7 reduce
  120.2 1.2 multiply_add_fusion
  121.4 11.2 %all-to-all-done.5 = bf16[32,8,512]{2,1,0:T(8,128)(2,1)S(1)} async-done(((bf16[32,8,512]{2,1,0:T(8,128)(2,1)}), bf16[32,8,512]{2,1,0:T(8,128)(2,1)S(1)}, u32[]{:S(2)}, u32[]{:S(2)}) %all-to-all-start.5) | async-done | bytes 262176 | tf_op jit(solution)/shard_map/all_to_all | solution.py:231
  132.6 0.9 event_rows.1
  (27 shorter events, 0.2 us)
Async XLA Ops:
  0.6 12.7 %copy-start.7 = (s32[1,128]{1,0:T(1,128)S(1)}, s32[1,128]{1,0:T(1,128)}, u32[]{:S(2)}) copy-start(s32[1,128]{1,0:T(1,128)} %param.14) | copy-start | bytes 1540
  0.6 12.7 %copy-start.5 = (s32[16,16]{1,0:T(8,128)S(1)}, s32[16,16]{1,0:T(8,128)}, u32[]{:S(2)}) copy-start(s32[16,16]{1,0:T(8,128)} %param.13) | copy-start | bytes 3076
  3.6 10.0 %copy-start.3 = (s32[16384]{0:T(1024)S(1)}, s32[16384]{0:T(1024)}, u32[]{:S(2)}) copy-start(s32[16384]{0:T(1024)} %param.16) | copy-start | bytes 196612
  3.6 10.1 %copy-start.4 = (s32[16384]{0:T(1024)S(1)}, s32[16384]{0:T(1024)}, u32[]{:S(2)}) copy-start(s32[16384]{0:T(1024)} %param.15) | copy-start | bytes 196612
  3.6 15.8 %all-to-all-start = ((bf16[16,192,128]{2,1,0:T(8,128)(2,1)}), bf16[16,192,128]{2,1,0:T(8,128)(2,1)S(1)}, u32[]{:S(2)}, u32[]{:S(2)}) async-start(bf16[16,192,128]{2,1,0:T(8,128)(2,1)} %project.1), calls=%async_computation | async-start | bytes 1572864 | tf_op jit(solution)/shard_map/all_to_all | solution.py:231
  13.7 21.2 %copy-start = (bf16[512,1536]{1,0:T(8,128)(2,1)S(1)}, bf16[512,1536]{1,0:T(8,128)(2,1)}, u32[]{:S(2)}) copy-start(bf16[512,1536]{1,0:T(8,128)(2,1)} %proj_ref.3) | copy-start | bytes 4718596
  23.7 11.2 %all-to-all-start.1 = ((bf16[16,128,128]{2,1,0:T(8,128)(2,1)}), bf16[16,128,128]{2,1,0:T(8,128)(2,1)S(1)}, u32[]{:S(2)}, u32[]{:S(2)}) async-start(bf16[16,128,128]{2,1,0:T(8,128)(2,1)} %attention.1), calls=%async_computation.1 | async-start | bytes 1048576 | tf_op jit(solution)/shard_map/all_to_all | solution.py:231
  77.1 22.0 %copy-start.6 = (f32[512]{0:T(512)S(1)}, f32[512]{0:T(512)}, u32[]{:S(2)}) copy-start(f32[512]{0:T(512)} %param.19) | copy-start | bytes 6148
  77.1 28.9 %copy-start.1 = (f32[512,512]{1,0:T(8,128)S(1)}, f32[512,512]{1,0:T(8,128)}, u32[]{:S(2)}) copy-start(f32[512,512]{1,0:T(8,128)} %moment_ref.1) | copy-start | bytes 3145732
  77.1 28.9 %copy-start.2 = (bf16[512,512]{1,0:T(8,128)(2,1)S(1)}, bf16[512,512]{1,0:T(8,128)(2,1)}, u32[]{:S(2)}) copy-start(bf16[512,512]{1,0:T(8,128)(2,1)} %table_ref.1) | copy-start | bytes 1572868
  91.9 14.1 %all-to-all-start.4 = ((bf16[16,32,512]{2,1,0:T(8,128)(2,1)}), bf16[16,32,512]{2,1,0:T(8,128)(2,1)S(1)}, u32[]{:S(2)}, u32[]{:S(2)}) async-start(bf16[16,32,512]{2,1,0:T(8,128)(2,1)} %row_sum.1), calls=%async_computation.4 | async-start | bytes 1048576 | tf_op jit(solution)/shard_map/all_to_all | solution.py:231
  107.5 25.1 %all-to-all-start.5 = ((bf16[32,8,512]{2,1,0:T(8,128)(2,1)}), bf16[32,8,512]{2,1,0:T(8,128)(2,1)S(1)}, u32[]{:S(2)}, u32[]{:S(2)}) async-start(bf16[32,8,512]{2,1,0:T(8,128)(2,1)} %bitcast.13), calls=%async_computation.5 | async-start | bytes 524288 | tf_op jit(solution)/shard_map/all_to_all | solution.py:231

commit v5 on v4

--- a/solution.py
+++ b/solution.py
@@ -192,7 +192,7 @@
 ):
     item_grad = grad_ref[...].astype(f32)
     mean = jnp.mean(item_grad * item_grad, axis=1, keepdims=True)
-    new_second = second_decay * second_ref[...] + (1.0 - second_decay) * mean
+    new_second = second_decay * second_ref[:, 0:1] + (1.0 - second_decay) * mean
     new_second_ref[...] = new_second
     rate = step_rate / (jnp.sqrt(new_second) + epsilon)
     new_moment = first_decay * moment_ref[...] + (1.0 - first_decay) * item_grad
@@ -253,6 +253,23 @@
     )(events_x[0], proj, out_grad[0])
     got = exchange(send, "seq", seq_shift)
 
+    place_of = owner_of * slab_rows + local_of
+    place = place_of[item_ids[0]]
+    owners = place // slab_rows
+    slab_index = place % slab_rows
+    event = jnp.arange(tokens)
+    earlier = (owners[:, None] == owners[None, :]) & (event[:, None] < event[None, :])
+    rank = jnp.sum(earlier.astype(jnp.int32), axis=0)
+    member = (owners - table_shift) % owner_count
+    target = (member * capacity + rank)[None, :]
+    lane = jnp.arange(LANES)[None, :]
+    digits = jnp.where(
+        lane == 0,
+        (slab_index // DIGIT + 1)[:, None],
+        jnp.where(lane == 1, (slab_index % DIGIT)[:, None], 0),
+    ).astype(bf16)
+    second_col = jnp.broadcast_to(second[:, None], (slab_rows, LANES))
+    got, target, digits, second_col = lax.optimization_barrier((got, target, digits, second_col))
     block_ids = jnp.arange(seq_count)
     visible = (block_mask == 1) | (block_ids[:, None] == block_ids[None, :])
     seen = jnp.repeat(visible.T.astype(f32), tokens, axis=1)
@@ -275,21 +292,6 @@
     )(part, seen, got)
     got_back = exchange(back, "seq", seq_shift)
 
-    place_of = owner_of * slab_rows + local_of
-    place = place_of[item_ids[0]]
-    owners = place // slab_rows
-    slab_index = place % slab_rows
-    event = jnp.arange(tokens)
-    earlier = (owners[:, None] == owners[None, :]) & (event[:, None] < event[None, :])
-    rank = jnp.sum(earlier.astype(jnp.int32), axis=0)
-    member = (owners - table_shift) % owner_count
-    target = (member * capacity + rank)[None, :]
-    lane = jnp.arange(LANES)[None, :]
-    digits = jnp.where(
-        lane == 0,
-        (slab_index // DIGIT + 1)[:, None],
-        jnp.where(lane == 1, (slab_index % DIGIT)[:, None], 0),
-    ).astype(bf16)
     send_rows = pl.pallas_call(
         functools.partial(input_grad_kernel, seq_shift),
         out_shape=shape((slots, features + LANES), bf16),
@@ -322,7 +324,7 @@
         in_specs=[
             whole((slab_rows, features)),
             whole((slab_rows, features)),
-            whole((slab_rows, 1)),
+            whole((slab_rows, LANES)),
             whole((slab_rows, features)),
             pl.BlockSpec((slots, LANES), lambda i: (0, features // LANES)),
         ],
@@ -332,7 +334,7 @@
             whole((slots, features)),
         ),
         compiler_params=limit(12), name="adam",
-    )(item_grad, moment, second[:, None], table, got_rows)
+    )(item_grad, moment, second_col, table, got_rows)
     new_moment = first_decay * moment + (1.0 - first_decay) * item_grad.astype(f32)
     returned = exchange(reply.reshape(owner_count, capacity, features), "table", table_shift)
     event_rows = pl.pallas_call(

time: 134 us -> 132 us (0.985)
  blocking collectives: 54.7 us -> 79.6 us
  starting transfers between devices: 36 us -> 21.7 us
  waiting for transfers between devices: 26.3 us -> 15.4 us
  Pallas kernels: 11.9 us -> 10.3 us
    all_to_all x2 -> x4, blocking collectives: 54.7 us -> 79.6 us  [exchange(): lax.all_to_all(array, axis, split_axis=0, concat_axis=0, axis_index_group...]
    all_to_all x4 -> x2, starting transfers between devices: 36 us -> 21.7 us  [exchange(): lax.all_to_all(array, axis, split_axis=0, concat_axis=0, axis_index_group...]
    all_to_all x4 -> x2, waiting for transfers between devices: 26.3 us -> 15.4 us  [exchange(): lax.all_to_all(array, axis, split_axis=0, concat_axis=0, axis_index_group...]
  transfers between devices with their start and end apart: 4 -> 2, of which waited for: 4 -> 2; matrix products, arithmetic and copies ran while one was open for 3% -> 3% of each run, Pallas kernels for 0% -> 0%
where the time goes in v5:
time: 132 us
  blocking collectives  79.6 us (60%)
  starting transfers between devices  21.7 us (16%)
  waiting for transfers between devices  15.4 us (12%)
  Pallas kernels  10.3 us (8%)
  other arithmetic  2.21 us (2%)
  local copies, waits for them, and re-layouts  1.51 us (1%)
    all_to_all x4, blocking collectives, exchange(): lax.all_to_all(array, axis, split_axis=0, concat_axis=0, axis_index_group...  79.6 us
    all_to_all x2, starting transfers between devices, exchange(): lax.all_to_all(array, axis, split_axis=0, concat_axis=0, axis_index_group...  21.7 us
    all_to_all x2, waiting for transfers between devices, exchange(): lax.all_to_all(array, axis, split_axis=0, concat_axis=0, axis_index_group...  15.4 us
    pallas_call x1, Pallas kernels, body(): pl.pallas_call(functools.partial(attention_kernel, seq_shift), out_shape=...  3.56 us
    pallas_call x1, Pallas kernels, body(): pl.pallas_call(functools.partial(project_kernel, seq_shift), out_shape=sh...  2.97 us
  transfers between devices with their start and end apart: 2, of which 2 were waited for; matrix products, arithmetic and copies ran while one was open for 3% of the time, Pallas kernels for 0%

profile of v5, /device:TPU:1, one launch (start us, length us, event | category | flops | bytes accessed | tf_op | source)
XLA Modules:
  0.0 131.6 jit_solution(16975933999592375576)
XLA Ops:
  0.7 3.0 %project.1 = bf16[16,192,128]{2,1,0:T(8,128)(2,1)} custom-call(bf16[128,512]{1,0:T(8,128)(2,1)} %bitcast.41, bf16[512,1536]{1,0:T(8,128)(2,1)} %proj_ref.3, bf16[128,512]{1,0:T(8,128)(2,1)} %bitcast.42), custom_call_target="tpu_custom_call" | custom-call | tf_op jit(solution)/shard_map/project/pallas_call | solution.py:249
  3.6 9.8 %all-to-all-start = ((bf16[16,192,128]{2,1,0:T(8,128)(2,1)}), bf16[16,192,128]{2,1,0:T(8,128)(2,1)S(1)}, u32[]{:S(2)}, u32[]{:S(2)}) async-start(bf16[16,192,128]{2,1,0:T(8,128)(2,1)} %project.1), calls=%async_computation | async-start | bytes 1572864 | tf_op jit(solution)/shard_map/all_to_all | solution.py:231
  13.5 0.1 copy.16
  13.6 1.1 gather_fusion
  14.7 0.1 convert_reduce_fusion
  14.9 0.1 broadcast_in_dim.42
  15.1 0.1 select_convert_fusion.digits_ref
  15.2 4.2 %all-to-all-done.got_ref = bf16[16,192,128]{2,1,0:T(8,128)(2,1)S(1)} async-done(((bf16[16,192,128]{2,1,0:T(8,128)(2,1)}), bf16[16,192,128]{2,1,0:T(8,128)(2,1)S(1)}, u32[]{:S(2)}, u32[]{:S(2)}) %all-to-all-start) | async-done | bytes 786464 | tf_op jit(solution)/shard_map/all_to_all | solution.py:231
  19.4 0.1 broadcast_in_dim.65.second_ref
  19.5 3.6 %attention.1 = bf16[16,128,128]{2,1,0:T(8,128)(2,1)S(1)} custom-call(s32[1]{0:T(128)} %bitcast.part_ref, f32[16,2048]{1,0:T(8,128)S(1)} %bitcast.39, bf16[16,192,128]{2,1,0:T(8,128)(2,1)S(1)} %all-to-all-done.got_ref), custom_call_target="tpu_custom_call" | custom-call | tf_op jit(solution)/shard_map/attention/pallas_call | solution.py:277
  23.1 11.0 %all_to_all.30.got_ref = bf16[16,128,128]{2,1,0:T(8,128)(2,1)S(1)} all-to-all(bf16[16,128,128]{2,1,0:T(8,128)(2,1)S(1)} %attention.1), channel_id=1, replica_groups={{320,352,384,416,448,480,0,32,64,96,128,160,192,224,256,288},{321,353,3..., dimensions={0} | all-to-all | bytes 1048576 | tf_op jit(solution)/shard_map/all_to_all | solution.py:231
  34.1 0.9 input_grad.1
  35.0 40.8 %all_to_all.31 = bf16[32,8,640]{2,1,0:T(8,128)(2,1)S(1)} all-to-all(bf16[32,8,640]{2,1,0:T(8,128)(2,1)S(1)} %bitcast.37), channel_id=1, replica_groups={{18,19,20,21,22,23,24,25,26,27,28,29,30,31,0,1,2,3,4,5,6,7,8,9,10,11,12..., dimensions={0} | all-to-all | bytes 655360 | tf_op jit(solution)/shard_map/all_to_all | solution.py:231
  75.8 0.5 slab.1
  76.3 0.0 copy-start.1
  76.3 13.8 %all_to_all.32.got_ref = bf16[16,32,512]{2,1,0:T(8,128)(2,1)S(1)} all-to-all(bf16[16,32,512]{2,1,0:T(8,128)(2,1)S(1)} %bitcast.36), channel_id=1, replica_groups={{320,352,384,416,448,480,0,32,64,96,128,160,192,224,256,288},{321,353,3..., dimensions={0} | all-to-all | bytes 1048576 | tf_op jit(solution)/shard_map/all_to_all | solution.py:231
  90.2 0.1 row_sum.1
  90.3 13.9 %all_to_all.33 = bf16[16,32,512]{2,1,0:T(8,128)(2,1)S(1)} all-to-all(bf16[16,32,512]{2,1,0:T(8,128)(2,1)S(1)} %row_sum.1), channel_id=1, replica_groups={{320,352,384,416,448,480,0,32,64,96,128,160,192,224,256,288},{321,353,3..., dimensions={0} | all-to-all | bytes 1048576 | tf_op jit(solution)/shard_map/all_to_all | solution.py:231
  104.2 1.5 %adam.1 = (bf16[512,512]{1,0:T(8,128)(2,1)}, f32[512,1]{1,0:T(8,128)S(1)}, bf16[256,512]{1,0:T(8,128)(2,1)}) custom-call(bf16[512,512]{1,0:T(8,128)(2,1)S(1)} %bitcast.33, f32[512,512]{1,0:T(8,128)S(1)} %copy-done.1, f32[512,128]{1,0:T(8,128)S(1)} %broadcast_in_dim.65.second_ref, bf16[512,512]{1,0:T(8,128)(2,1)S(1)} %copy-done.2, bf16[256,640]{1,0:T(8,128)(2,1)S(1)} %bitcast.35), custom_call_target="tpu_custom_call" | custom-call | tf_op jit(solution)/shard_map/adam/pallas_call | solution.py:316
  105.7 12.0 %all-to-all-start.5 = ((bf16[32,8,512]{2,1,0:T(8,128)(2,1)}), bf16[32,8,512]{2,1,0:T(8,128)(2,1)S(1)}, u32[]{:S(2)}, u32[]{:S(2)}) async-start(bf16[32,8,512]{2,1,0:T(8,128)(2,1)} %bitcast.12), calls=%async_computation.5 | async-start | bytes 524288 | tf_op jit(solution)/shard_map/all_to_all | solution.py:231
  117.7 0.7 reduce
  118.4 1.2 multiply_add_fusion
  119.6 11.2 %all-to-all-done.5 = bf16[32,8,512]{2,1,0:T(8,128)(2,1)S(1)} async-done(((bf16[32,8,512]{2,1,0:T(8,128)(2,1)}), bf16[32,8,512]{2,1,0:T(8,128)(2,1)S(1)}, u32[]{:S(2)}, u32[]{:S(2)}) %all-to-all-start.5) | async-done | bytes 262176 | tf_op jit(solution)/shard_map/all_to_all | solution.py:231
  130.8 0.9 event_rows.1
  (25 shorter events, 0.2 us)
Async XLA Ops:
  0.6 12.8 %copy-start.7 = (s32[1,128]{1,0:T(1,128)S(1)}, s32[1,128]{1,0:T(1,128)}, u32[]{:S(2)}) copy-start(s32[1,128]{1,0:T(1,128)} %param.14) | copy-start | bytes 1540
  0.6 12.8 %copy-start.5 = (s32[16,16]{1,0:T(8,128)S(1)}, s32[16,16]{1,0:T(8,128)}, u32[]{:S(2)}) copy-start(s32[16,16]{1,0:T(8,128)} %param.13) | copy-start | bytes 3076
  0.7 12.9 %copy-start.3 = (s32[16384]{0:T(1024)S(1)}, s32[16384]{0:T(1024)}, u32[]{:S(2)}) copy-start(s32[16384]{0:T(1024)} %param.16) | copy-start | bytes 196612
  0.7 12.9 %copy-start.4 = (s32[16384]{0:T(1024)S(1)}, s32[16384]{0:T(1024)}, u32[]{:S(2)}) copy-start(s32[16384]{0:T(1024)} %param.15) | copy-start | bytes 196612
  3.6 15.8 %copy-start.6 = (f32[512]{0:T(512)S(1)}, f32[512]{0:T(512)}, u32[]{:S(2)}) copy-start(f32[512]{0:T(512)} %param.19) | copy-start | bytes 6148
  3.6 15.8 %all-to-all-start = ((bf16[16,192,128]{2,1,0:T(8,128)(2,1)}), bf16[16,192,128]{2,1,0:T(8,128)(2,1)S(1)}, u32[]{:S(2)}, u32[]{:S(2)}) async-start(bf16[16,192,128]{2,1,0:T(8,128)(2,1)} %project.1), calls=%async_computation | async-start | bytes 1572864 | tf_op jit(solution)/shard_map/all_to_all | solution.py:231
  14.8 19.3 %copy-start = (bf16[512,1536]{1,0:T(8,128)(2,1)S(1)}, bf16[512,1536]{1,0:T(8,128)(2,1)}, u32[]{:S(2)}) copy-start(bf16[512,1536]{1,0:T(8,128)(2,1)} %proj_ref.3) | copy-start | bytes 4718596
  76.3 27.9 %copy-start.1 = (f32[512,512]{1,0:T(8,128)S(1)}, f32[512,512]{1,0:T(8,128)}, u32[]{:S(2)}) copy-start(f32[512,512]{1,0:T(8,128)} %moment_ref.1) | copy-start | bytes 3145732
  76.3 27.9 %copy-start.2 = (bf16[512,512]{1,0:T(8,128)(2,1)S(1)}, bf16[512,512]{1,0:T(8,128)(2,1)}, u32[]{:S(2)}) copy-start(bf16[512,512]{1,0:T(8,128)(2,1)} %table_ref.1) | copy-start | bytes 1572868
  105.7 25.1 %all-to-all-start.5 = ((bf16[32,8,512]{2,1,0:T(8,128)(2,1)}), bf16[32,8,512]{2,1,0:T(8,128)(2,1)S(1)}, u32[]{:S(2)}, u32[]{:S(2)}) async-start(bf16[32,8,512]{2,1,0:T(8,128)(2,1)} %bitcast.12), calls=%async_computation.5 | async-start | bytes 524288 | tf_op jit(solution)/shard_map/all_to_all | solution.py:231

commit v6 on v5

--- a/solution.py
+++ b/solution.py
@@ -130,7 +130,7 @@
         ).astype(bf16)
 
 
-def input_grad_kernel(shift, got_ref, proj_ref, target_ref, digits_ref, send_ref):
+def input_grad_kernel(shift, got_ref, proj_ref, target_ref, quarter_ref, digits_ref, send_ref):
     count, rows = got_ref.shape[0:2]
     half = rows // 2
     queries, keys, values = [], [], []
@@ -153,13 +153,20 @@
     input_grad = lax.dot_general(
         stacked, proj_ref[...], (((1,), (1,)), ((), ())), preferred_element_type=f32
     ).astype(bf16)
-    slots = send_ref.shape[0]
-    features = input_grad.shape[1]
-    onehot = (
-        lax.broadcasted_iota(jnp.int32, (slots, rows), 0) == target_ref[...]
-    ).astype(f32).astype(bf16)
-    send_ref[:, 0:features] = jnp.dot(onehot, input_grad, preferred_element_type=f32).astype(bf16)
-    send_ref[:, features:] = jnp.dot(onehot, digits_ref[...], preferred_element_type=f32).astype(bf16)
+    owners, pieces, lines = send_ref.shape[0:3]
+    groups = (pieces - 1) * LANES // input_grad.shape[1]
+    slots = groups * owners * lines
+
+    def placed(at_ref, places, values):
+        onehot = lax.broadcasted_iota(jnp.int32, (places, rows), 0) == at_ref[...]
+        return jnp.dot(onehot.astype(f32).astype(bf16), values, preferred_element_type=f32)
+
+    send_rows = placed(target_ref, slots, input_grad).reshape(owners, groups, lines, -1)
+    for piece in range(pieces - 1):
+        at = piece // groups * LANES
+        send_ref[:, piece] = send_rows[:, piece % groups, :, at : at + LANES].astype(bf16)
+    digits = placed(quarter_ref, slots // groups, digits_ref[...]).reshape(owners, lines, LANES)
+    send_ref[:, pieces - 1] = digits.astype(bf16)
 
 
 def slot_rows(digits, slab_rows):
@@ -169,12 +176,24 @@
     return (row == lane).astype(f32).astype(bf16)
 
 
-def slab_kernel(got_ref, slab_ref):
+def slab_kernel(got_ref, slab_ref, digits_ref):
+    owners, pieces, lines = got_ref.shape[0:3]
     slab_rows, features = slab_ref.shape
-    select = slot_rows(got_ref[:, features:], slab_rows)
-    slab_ref[...] = lax.dot_general(
-        select, got_ref[:, 0:features], (((0,), (0,)), ((), ())), preferred_element_type=f32
-    ).astype(bf16)
+    groups = (pieces - 1) * LANES // features
+    first = got_ref[:, pieces - 1].astype(f32).reshape(owners * lines, LANES)
+    spread = [first]
+    for group in range(1, groups):
+        spread.append(pltpu.roll(first, LANES - 2 * group, 1))
+    spread = [digits.reshape(owners, lines, LANES) for digits in spread]
+    digits = jnp.concatenate(spread, axis=1).reshape(groups * owners * lines, LANES).astype(bf16)
+    digits_ref[...] = digits
+    select = slot_rows(digits, slab_rows)
+    for column in range(features // LANES):
+        parts = [got_ref[:, groups * column + group].astype(f32) for group in range(groups)]
+        got = jnp.concatenate(parts, axis=1).reshape(digits.shape).astype(bf16)
+        slab_ref[:, column * LANES : column * LANES + LANES] = lax.dot_general(
+            select, got, (((0,), (0,)), ((), ())), preferred_element_type=f32
+        ).astype(bf16)
 
 
 def sum_kernel(got_ref, out_ref):
@@ -262,14 +281,21 @@
     rank = jnp.sum(earlier.astype(jnp.int32), axis=0)
     member = (owners - table_shift) % owner_count
     target = (member * capacity + rank)[None, :]
+    groups = 4
+    lines = capacity // groups
+    quarter = (member * lines + rank % lines)[None, :]
+    pieces = groups * (features // LANES) + 1
+    first_lane = 2 * (rank // lines)
     lane = jnp.arange(LANES)[None, :]
     digits = jnp.where(
-        lane == 0,
+        lane == first_lane[:, None],
         (slab_index // DIGIT + 1)[:, None],
-        jnp.where(lane == 1, (slab_index % DIGIT)[:, None], 0),
+        jnp.where(lane == first_lane[:, None] + 1, (slab_index % DIGIT)[:, None], 0),
     ).astype(bf16)
     second_col = jnp.broadcast_to(second[:, None], (slab_rows, LANES))
-    got, target, digits, second_col = lax.optimization_barrier((got, target, digits, second_col))
+    got, target, quarter, digits, second_col = lax.optimization_barrier(
+        (got, target, quarter, digits, second_col)
+    )
     block_ids = jnp.arange(seq_count)
     visible = (block_mask == 1) | (block_ids[:, None] == block_ids[None, :])
     seen = jnp.repeat(visible.T.astype(f32), tokens, axis=1)
@@ -294,16 +320,16 @@
 
     send_rows = pl.pallas_call(
         functools.partial(input_grad_kernel, seq_shift),
-        out_shape=shape((slots, features + LANES), bf16),
+        out_shape=shape((owner_count, pieces, lines, LANES), bf16),
         compiler_params=limit(12), name="input_grad",
-    )(got_back, proj, target, digits)
-    got_rows = exchange(
-        send_rows.reshape(owner_count, capacity, features + LANES), "table", table_shift
-    ).reshape(slots, features + LANES)
-
-    slab = pl.pallas_call(slab_kernel, out_shape=shape((slab_rows, features), bf16), compiler_params=limit(8), name="slab")(
-        got_rows
-    )
+    )(got_back, proj, target, quarter, digits)
+    got_rows = exchange(send_rows, "table", table_shift)
+
+    slab, got_digits = pl.pallas_call(
+        slab_kernel,
+        out_shape=(shape((slab_rows, features), bf16), shape((slots, LANES), bf16)),
+        compiler_params=limit(8), name="slab",
+    )(got_rows)
     share = slab_rows // seq_count
     parts = exchange(slab.reshape(seq_count, share, features), "seq", seq_shift)
     copies = pl.pallas_call(
@@ -326,7 +352,7 @@
             whole((slab_rows, features)),
             whole((slab_rows, LANES)),
             whole((slab_rows, features)),
-            pl.BlockSpec((slots, LANES), lambda i: (0, features // LANES)),
+            whole((slots, LANES)),
         ],
         out_specs=(
             whole((slab_rows, features)),
@@ -334,7 +360,7 @@
             whole((slots, features)),
         ),
         compiler_params=limit(12), name="adam",
-    )(item_grad, moment, second_col, table, got_rows)
+    )(item_grad, moment, second_col, table, got_digits)
     new_moment = first_decay * moment + (1.0 - first_decay) * item_grad.astype(f32)
     returned = exchange(reply.reshape(owner_count, capacity, features), "table", table_shift)
     event_rows = pl.pallas_call(

time: 132 us -> 130 us (0.985)
  blocking collectives: 79.6 us -> 77.4 us
    all_to_all x4, blocking collectives: 79.6 us -> 77.4 us  [exchange(): lax.all_to_all(array, axis, split_axis=0, concat_axis=0, axis_index_group...]
where the time goes in v6:
time: 130 us
  blocking collectives  77.4 us (60%)
  starting transfers between devices  21.7 us (17%)
  waiting for transfers between devices  15.4 us (12%)
  Pallas kernels  10.8 us (8%)
  other arithmetic  2.26 us (2%)
  local copies, waits for them, and re-layouts  1.51 us (1%)
    all_to_all x4, blocking collectives, exchange(): lax.all_to_all(array, axis, split_axis=0, concat_axis=0, axis_index_group...  77.4 us
    all_to_all x2, starting transfers between devices, exchange(): lax.all_to_all(array, axis, split_axis=0, concat_axis=0, axis_index_group...  21.7 us
    all_to_all x2, waiting for transfers between devices, exchange(): lax.all_to_all(array, axis, split_axis=0, concat_axis=0, axis_index_group...  15.4 us
    pallas_call x1, Pallas kernels, body(): pl.pallas_call(functools.partial(attention_kernel, seq_shift), out_shape=...  3.56 us
    pallas_call x1, Pallas kernels, body(): pl.pallas_call(functools.partial(project_kernel, seq_shift), out_shape=sh...  2.97 us
  transfers between devices with their start and end apart: 2, of which 2 were waited for; matrix products, arithmetic and copies ran while one was open for 3% of the time, Pallas kernels for 0%

profile of v6, /device:TPU:1, one launch (start us, length us, event | category | flops | bytes accessed | tf_op | source)
XLA Modules:
  0.0 129.8 jit_solution(5656957730284345559)
XLA Ops:
  0.7 3.0 %project.1 = bf16[16,192,128]{2,1,0:T(8,128)(2,1)} custom-call(bf16[128,512]{1,0:T(8,128)(2,1)} %bitcast.41, bf16[512,1536]{1,0:T(8,128)(2,1)} %proj_ref.3, bf16[128,512]{1,0:T(8,128)(2,1)} %bitcast.42), custom_call_target="tpu_custom_call" | custom-call | tf_op jit(solution)/shard_map/project/pallas_call | solution.py:268
  3.6 9.8 %all-to-all-start = ((bf16[16,192,128]{2,1,0:T(8,128)(2,1)}), bf16[16,192,128]{2,1,0:T(8,128)(2,1)S(1)}, u32[]{:S(2)}, u32[]{:S(2)}) async-start(bf16[16,192,128]{2,1,0:T(8,128)(2,1)} %project.1), calls=%async_computation | async-start | bytes 1572864 | tf_op jit(solution)/shard_map/all_to_all | solution.py:250
  13.5 0.1 copy.16
  13.6 1.1 gather_fusion
  14.8 0.1 broadcast_in_dim.26
  14.9 0.0 copy-start
  14.9 0.1 convert_reduce_fusion
  15.1 0.1 select_convert_fusion.digits_ref
  15.2 4.2 %all-to-all-done.got_ref = bf16[16,192,128]{2,1,0:T(8,128)(2,1)S(1)} async-done(((bf16[16,192,128]{2,1,0:T(8,128)(2,1)}), bf16[16,192,128]{2,1,0:T(8,128)(2,1)S(1)}, u32[]{:S(2)}, u32[]{:S(2)}) %all-to-all-start) | async-done | bytes 786464 | tf_op jit(solution)/shard_map/all_to_all | solution.py:250
  19.4 0.1 broadcast_in_dim.30.second_ref
  19.5 3.6 %attention.1 = bf16[16,128,128]{2,1,0:T(8,128)(2,1)S(1)} custom-call(s32[1]{0:T(128)} %bitcast.part_ref, f32[16,2048]{1,0:T(8,128)S(1)} %bitcast.39, bf16[16,192,128]{2,1,0:T(8,128)(2,1)S(1)} %all-to-all-done.got_ref), custom_call_target="tpu_custom_call" | custom-call | tf_op jit(solution)/shard_map/attention/pallas_call | solution.py:303
  23.1 11.0 %all_to_all.30.got_ref = bf16[16,128,128]{2,1,0:T(8,128)(2,1)S(1)} all-to-all(bf16[16,128,128]{2,1,0:T(8,128)(2,1)S(1)} %attention.1), channel_id=1, replica_groups={{320,352,384,416,448,480,0,32,64,96,128,160,192,224,256,288},{321,353,3..., dimensions={0} | all-to-all | bytes 1048576 | tf_op jit(solution)/shard_map/all_to_all | solution.py:250
  34.1 1.0 input_grad.1
  35.1 38.7 %all_to_all.31.got_ref = bf16[32,17,2,128]{3,2,1,0:T(2,128)(2,1)S(1)} all-to-all(bf16[32,17,2,128]{3,2,1,0:T(2,128)(2,1)S(1)} %input_grad.1), channel_id=1, replica_groups={{18,19,20,21,22,23,24,25,26,27,28,29,30,31,0,1,2,3,4,5,6,7,8,9,10,11,12..., dimensions={0} | all-to-all | bytes 557056 | tf_op jit(solution)/shard_map/all_to_all | solution.py:250
  73.8 0.8 slab.1
  74.6 13.8 %all_to_all.32.got_ref = bf16[16,32,512]{2,1,0:T(8,128)(2,1)S(1)} all-to-all(bf16[16,32,512]{2,1,0:T(8,128)(2,1)S(1)} %bitcast.38), channel_id=1, replica_groups={{320,352,384,416,448,480,0,32,64,96,128,160,192,224,256,288},{321,353,3..., dimensions={0} | all-to-all | bytes 1048576 | tf_op jit(solution)/shard_map/all_to_all | solution.py:250
  88.4 0.1 row_sum.1
  88.5 13.9 %all_to_all.33 = bf16[16,32,512]{2,1,0:T(8,128)(2,1)S(1)} all-to-all(bf16[16,32,512]{2,1,0:T(8,128)(2,1)S(1)} %row_sum.1), channel_id=1, replica_groups={{320,352,384,416,448,480,0,32,64,96,128,160,192,224,256,288},{321,353,3..., dimensions={0} | all-to-all | bytes 1048576 | tf_op jit(solution)/shard_map/all_to_all | solution.py:250
  102.4 1.5 %adam.1 = (bf16[512,512]{1,0:T(8,128)(2,1)}, f32[512,1]{1,0:T(8,128)S(1)}, bf16[256,512]{1,0:T(8,128)(2,1)}) custom-call(bf16[512,512]{1,0:T(8,128)(2,1)S(1)} %bitcast.36, f32[512,512]{1,0:T(8,128)S(1)} %copy-done.1, f32[512,128]{1,0:T(8,128)S(1)} %broadcast_in_dim.30.second_ref, bf16[512,512]{1,0:T(8,128)(2,1)S(1)} %copy-done.2, ...), custom_call_target="tpu_custom_call" | custom-call | tf_op jit(solution)/shard_map/adam/pallas_call | solution.py:342
  103.9 11.9 %all-to-all-start.5 = ((bf16[32,8,512]{2,1,0:T(8,128)(2,1)}), bf16[32,8,512]{2,1,0:T(8,128)(2,1)S(1)}, u32[]{:S(2)}, u32[]{:S(2)}) async-start(bf16[32,8,512]{2,1,0:T(8,128)(2,1)} %bitcast.10), calls=%async_computation.5 | async-start | bytes 524288 | tf_op jit(solution)/shard_map/all_to_all | solution.py:250
  115.8 0.7 reduce
  116.6 1.2 multiply_add_fusion
  117.8 11.2 %all-to-all-done.5 = bf16[32,8,512]{2,1,0:T(8,128)(2,1)S(1)} async-done(((bf16[32,8,512]{2,1,0:T(8,128)(2,1)}), bf16[32,8,512]{2,1,0:T(8,128)(2,1)S(1)}, u32[]{:S(2)}, u32[]{:S(2)}) %all-to-all-start.5) | async-done | bytes 262176 | tf_op jit(solution)/shard_map/all_to_all | solution.py:250
  129.0 0.9 event_rows.1
  (25 shorter events, 0.2 us)
Async XLA Ops:
  0.6 12.8 %copy-start.7 = (s32[1,128]{1,0:T(1,128)S(1)}, s32[1,128]{1,0:T(1,128)}, u32[]{:S(2)}) copy-start(s32[1,128]{1,0:T(1,128)} %param.14) | copy-start | bytes 1540
  0.6 12.8 %copy-start.5 = (s32[16,16]{1,0:T(8,128)S(1)}, s32[16,16]{1,0:T(8,128)}, u32[]{:S(2)}) copy-start(s32[16,16]{1,0:T(8,128)} %param.13) | copy-start | bytes 3076
  0.7 12.9 %copy-start.3 = (s32[16384]{0:T(1024)S(1)}, s32[16384]{0:T(1024)}, u32[]{:S(2)}) copy-start(s32[16384]{0:T(1024)} %param.16) | copy-start | bytes 196612
  0.7 12.9 %copy-start.4 = (s32[16384]{0:T(1024)S(1)}, s32[16384]{0:T(1024)}, u32[]{:S(2)}) copy-start(s32[16384]{0:T(1024)} %param.15) | copy-start | bytes 196612
  3.6 15.8 %copy-start.6 = (f32[512]{0:T(512)S(1)}, f32[512]{0:T(512)}, u32[]{:S(2)}) copy-start(f32[512]{0:T(512)} %param.19) | copy-start | bytes 6148
  3.6 15.8 %all-to-all-start = ((bf16[16,192,128]{2,1,0:T(8,128)(2,1)}), bf16[16,192,128]{2,1,0:T(8,128)(2,1)S(1)}, u32[]{:S(2)}, u32[]{:S(2)}) async-start(bf16[16,192,128]{2,1,0:T(8,128)(2,1)} %project.1), calls=%async_computation | async-start | bytes 1572864 | tf_op jit(solution)/shard_map/all_to_all | solution.py:250
  14.9 19.3 %copy-start = (bf16[512,1536]{1,0:T(8,128)(2,1)S(1)}, bf16[512,1536]{1,0:T(8,128)(2,1)}, u32[]{:S(2)}) copy-start(bf16[512,1536]{1,0:T(8,128)(2,1)} %proj_ref.3) | copy-start | bytes 4718596
  74.6 27.8 %copy-start.1 = (f32[512,512]{1,0:T(8,128)S(1)}, f32[512,512]{1,0:T(8,128)}, u32[]{:S(2)}) copy-start(f32[512,512]{1,0:T(8,128)} %moment_ref.1) | copy-start | bytes 3145732
  74.6 27.8 %copy-start.2 = (bf16[512,512]{1,0:T(8,128)(2,1)S(1)}, bf16[512,512]{1,0:T(8,128)(2,1)}, u32[]{:S(2)}) copy-start(bf16[512,512]{1,0:T(8,128)(2,1)} %table_ref.1) | copy-start | bytes 1572868
  103.9 25.1 %all-to-all-start.5 = ((bf16[32,8,512]{2,1,0:T(8,128)(2,1)}), bf16[32,8,512]{2,1,0:T(8,128)(2,1)S(1)}, u32[]{:S(2)}, u32[]{:S(2)}) async-start(bf16[32,8,512]{2,1,0:T(8,128)(2,1)} %bitcast.10), calls=%async_computation.5 | async-start | bytes 524288 | tf_op jit(solution)/shard_map/all_to_all | solution.py:250

commit v7 on v6

--- a/solution.py
+++ b/solution.py
@@ -207,14 +207,16 @@
 
 
 def adam_kernel(
-    grad_ref, moment_ref, second_ref, table_ref, digits_ref, new_table_ref, new_second_ref, reply_ref
+    grad_ref, moment_ref, second_ref, table_ref, digits_ref,
+    new_table_ref, new_moment_ref, new_second_ref, reply_ref,
 ):
     item_grad = grad_ref[...].astype(f32)
     mean = jnp.mean(item_grad * item_grad, axis=1, keepdims=True)
     new_second = second_decay * second_ref[:, 0:1] + (1.0 - second_decay) * mean
-    new_second_ref[...] = new_second
+    new_second_ref[...] = jnp.broadcast_to(new_second, second_ref.shape).T[0:1]
     rate = step_rate / (jnp.sqrt(new_second) + epsilon)
     new_moment = first_decay * moment_ref[...] + (1.0 - first_decay) * item_grad
+    new_moment_ref[...] = new_moment
     new_table = (table_ref[...].astype(f32) - new_moment * rate).astype(bf16)
     new_table_ref[...] = new_table
     select = slot_rows(digits_ref[...], new_table.shape[0])
@@ -263,7 +265,7 @@
     slots = owner_count * capacity
     half = tokens // 2
     seq_shift = seq_count // 2 + math.isqrt(seq_count) // 2
-    table_shift = owner_count // 2 + 2
+    table_shift = owner_count // 2 + 3
 
     send = pl.pallas_call(
         functools.partial(project_kernel, seq_shift),
@@ -339,11 +341,12 @@
     )(parts)
     item_grad = exchange(copies, "seq", seq_shift).reshape(slab_rows, features)
 
-    new_table, new_second, reply = pl.pallas_call(
+    new_table, new_moment, new_second, reply = pl.pallas_call(
         adam_kernel,
         out_shape=(
             shape((slab_rows, features), bf16),
-            shape((slab_rows, 1), f32),
+            shape((slab_rows, features), f32),
+            shape((1, slab_rows), f32),
             shape((slots, features), bf16),
         ),
         grid=(1,),
@@ -356,19 +359,19 @@
         ],
         out_specs=(
             whole((slab_rows, features)),
-            whole((slab_rows, 1)),
+            whole((slab_rows, features)),
+            whole((1, slab_rows)),
             whole((slots, features)),
         ),
         compiler_params=limit(12), name="adam",
     )(item_grad, moment, second_col, table, got_digits)
-    new_moment = first_decay * moment + (1.0 - first_decay) * item_grad.astype(f32)
     returned = exchange(reply.reshape(owner_count, capacity, features), "table", table_shift)
     event_rows = pl.pallas_call(
         event_kernel,
         out_shape=shape((tokens, features), bf16),
         compiler_params=limit(8), name="event_rows",
     )(target, returned.reshape(slots, features))
-    return (new_table, new_moment, new_second[:, 0], event_rows[None])
+    return (new_table, new_moment, new_second[0], event_rows[None])
 
 
 def solution(mesh):

time: 130 us -> 130 us (level)
  blocking collectives: 77.4 us -> 102 us
  starting transfers between devices: 21.7 us -> 9.76 us
  waiting for transfers between devices: 15.4 us -> 4.19 us
  other arithmetic: 2.26 us -> 0.33 us
    all_to_all x4 -> x5, blocking collectives: 77.4 us -> 102 us  [exchange(): lax.all_to_all(array, axis, split_axis=0, concat_axis=0, axis_index_group...]
    all_to_all x2 -> x1, starting transfers between devices: 21.7 us -> 9.76 us  [exchange(): lax.all_to_all(array, axis, split_axis=0, concat_axis=0, axis_index_group...]
    all_to_all x2 -> x1, waiting for transfers between devices: 15.4 us -> 4.19 us  [exchange(): lax.all_to_all(array, axis, split_axis=0, concat_axis=0, axis_index_group...]
  transfers between devices with their start and end apart: 2 -> 1, of which waited for: 2 -> 1; matrix products, arithmetic and copies ran while one was open for 3% -> 1% of each run, Pallas kernels for 0% -> 0%
where the time goes in v7:
time: 130 us; the launch traced here: 129 us
  blocking collectives  102 us (78%)
  Pallas kernels  11 us (8%)
  starting transfers between devices  9.76 us (8%)
  waiting for transfers between devices  4.19 us (3%)
  local copies, waits for them, and re-layouts  1.51 us (1%)
    all_to_all x5, blocking collectives, exchange(): lax.all_to_all(array, axis, split_axis=0, concat_axis=0, axis_index_group...  102 us
    all_to_all x1, starting transfers between devices, exchange(): lax.all_to_all(array, axis, split_axis=0, concat_axis=0, axis_index_group...  9.76 us
    all_to_all x1, waiting for transfers between devices, exchange(): lax.all_to_all(array, axis, split_axis=0, concat_axis=0, axis_index_group...  4.19 us
    pallas_call x1, Pallas kernels, body(): pl.pallas_call(functools.partial(attention_kernel, seq_shift), out_shape=...  3.53 us
    pallas_call x1, Pallas kernels, body(): pl.pallas_call(functools.partial(project_kernel, seq_shift), out_shape=sh...  2.97 us
  transfers between devices with their start and end apart: 1, of which 1 were waited for; matrix products, arithmetic and copies ran while one was open for 1% of the time, Pallas kernels for 0%

profile of v7, /device:TPU:1, one launch (start us, length us, event | category | flops | bytes accessed | tf_op | source)
XLA Modules:
  0.0 129.4 jit_solution(486208514496199568)
XLA Ops:
  0.7 3.0 %project.1 = bf16[16,192,128]{2,1,0:T(8,128)(2,1)} custom-call(bf16[128,512]{1,0:T(8,128)(2,1)} %bitcast.42, bf16[512,1536]{1,0:T(8,128)(2,1)} %proj_ref.3, bf16[128,512]{1,0:T(8,128)(2,1)} %bitcast.43), custom_call_target="tpu_custom_call" | custom-call | tf_op jit(solution)/shard_map/project/pallas_call | solution.py:270
  3.6 9.8 %all-to-all-start = ((bf16[16,192,128]{2,1,0:T(8,128)(2,1)}), bf16[16,192,128]{2,1,0:T(8,128)(2,1)S(1)}, u32[]{:S(2)}, u32[]{:S(2)}) async-start(bf16[16,192,128]{2,1,0:T(8,128)(2,1)} %project.1), calls=%async_computation | async-start | bytes 1572864 | tf_op jit(solution)/shard_map/all_to_all | solution.py:252
  13.5 0.1 copy.16
  13.5 0.0 copy-done.4
  13.6 1.1 gather_fusion
  14.8 0.1 broadcast_in_dim.26
  14.9 0.0 copy-start
  14.9 0.1 convert_reduce_fusion
  15.1 0.1 select_convert_fusion.digits_ref
  15.2 4.2 %all-to-all-done.got_ref = bf16[16,192,128]{2,1,0:T(8,128)(2,1)S(1)} async-done(((bf16[16,192,128]{2,1,0:T(8,128)(2,1)}), bf16[16,192,128]{2,1,0:T(8,128)(2,1)S(1)}, u32[]{:S(2)}, u32[]{:S(2)}) %all-to-all-start) | async-done | bytes 786464 | tf_op jit(solution)/shard_map/all_to_all | solution.py:252
  19.4 0.1 broadcast_in_dim.30.second_ref
  19.5 3.5 %attention.1 = bf16[16,128,128]{2,1,0:T(8,128)(2,1)S(1)} custom-call(s32[1]{0:T(128)} %bitcast.part_ref, f32[16,2048]{1,0:T(8,128)S(1)} %bitcast.39, bf16[16,192,128]{2,1,0:T(8,128)(2,1)S(1)} %all-to-all-done.got_ref), custom_call_target="tpu_custom_call" | custom-call | tf_op jit(solution)/shard_map/attention/pallas_call | solution.py:305
  23.1 11.0 %all_to_all.30.got_ref = bf16[16,128,128]{2,1,0:T(8,128)(2,1)S(1)} all-to-all(bf16[16,128,128]{2,1,0:T(8,128)(2,1)S(1)} %attention.1), channel_id=1, replica_groups={{320,352,384,416,448,480,0,32,64,96,128,160,192,224,256,288},{321,353,3..., dimensions={0} | all-to-all | bytes 1048576 | tf_op jit(solution)/shard_map/all_to_all | solution.py:252
  34.1 1.0 input_grad.1
  35.1 38.4 %all_to_all.31.got_ref = bf16[32,17,2,128]{3,2,1,0:T(2,128)(2,1)S(1)} all-to-all(bf16[32,17,2,128]{3,2,1,0:T(2,128)(2,1)S(1)} %input_grad.1), channel_id=1, replica_groups={{19,20,21,22,23,24,25,26,27,28,29,30,31,0,1,2,3,4,5,6,7,8,9,10,11,12,13..., dimensions={0} | all-to-all | bytes 557056 | tf_op jit(solution)/shard_map/all_to_all | solution.py:252
  73.4 0.8 slab.1
  74.2 0.0 copy-start.1
  74.3 0.0 copy-start.2
  74.3 13.4 %all_to_all.32.got_ref = bf16[16,32,512]{2,1,0:T(8,128)(2,1)S(1)} all-to-all(bf16[16,32,512]{2,1,0:T(8,128)(2,1)S(1)} %bitcast.38), channel_id=1, replica_groups={{320,352,384,416,448,480,0,32,64,96,128,160,192,224,256,288},{321,353,3..., dimensions={0} | all-to-all | bytes 1048576 | tf_op jit(solution)/shard_map/all_to_all | solution.py:252
  87.7 0.1 row_sum.1
  87.8 13.4 %all_to_all.33 = bf16[16,32,512]{2,1,0:T(8,128)(2,1)S(1)} all-to-all(bf16[16,32,512]{2,1,0:T(8,128)(2,1)S(1)} %row_sum.1), channel_id=1, replica_groups={{320,352,384,416,448,480,0,32,64,96,128,160,192,224,256,288},{321,353,3..., dimensions={0} | all-to-all | bytes 1048576 | tf_op jit(solution)/shard_map/all_to_all | solution.py:252
  101.2 1.8 %adam.1 = (bf16[512,512]{1,0:T(8,128)(2,1)}, f32[512,512]{1,0:T(8,128)}, f32[1,512]{1,0:T(1,128)}, bf16[256,512]{1,0:T(8,128)(2,1)S(1)}) custom-call(bf16[512,512]{1,0:T(8,128)(2,1)S(1)} %bitcast.36, f32[512,512]{1,0:T(8,128)S(1)} %copy-done.1, f32[512,128]{1,0:T(8,128)S(1)} %broadcast_in_dim.30.second_ref, bf16[512,512]{1,0:T(8,128)(2,1)S(1)} %copy-done.2, ...), custom_call_target="tpu_custom_call" | custom-call | tf_op jit(solution)/shard_map/adam/pallas_call | solution.py:344
  103.0 25.5 %all_to_all.34 = bf16[32,8,512]{2,1,0:T(8,128)(2,1)S(1)} all-to-all(bf16[32,8,512]{2,1,0:T(8,128)(2,1)S(1)} %bitcast.40), channel_id=1, replica_groups={{19,20,21,22,23,24,25,26,27,28,29,30,31,0,1,2,3,4,5,6,7,8,9,10,11,12,13..., dimensions={0} | all-to-all | bytes 524288 | tf_op jit(solution)/shard_map/all_to_all | solution.py:252
  128.5 0.9 event_rows.1
  (22 shorter events, 0.2 us)
Async XLA Ops:
  0.6 12.8 %copy-start.7 = (s32[1,128]{1,0:T(1,128)S(1)}, s32[1,128]{1,0:T(1,128)}, u32[]{:S(2)}) copy-start(s32[1,128]{1,0:T(1,128)} %param.14) | copy-start | bytes 1540
  0.6 12.8 %copy-start.5 = (s32[16,16]{1,0:T(8,128)S(1)}, s32[16,16]{1,0:T(8,128)}, u32[]{:S(2)}) copy-start(s32[16,16]{1,0:T(8,128)} %param.13) | copy-start | bytes 3076
  0.7 12.9 %copy-start.3 = (s32[16384]{0:T(1024)S(1)}, s32[16384]{0:T(1024)}, u32[]{:S(2)}) copy-start(s32[16384]{0:T(1024)} %param.16) | copy-start | bytes 196612
  0.7 12.9 %copy-start.4 = (s32[16384]{0:T(1024)S(1)}, s32[16384]{0:T(1024)}, u32[]{:S(2)}) copy-start(s32[16384]{0:T(1024)} %param.15) | copy-start | bytes 196612
  3.6 15.8 %copy-start.6 = (f32[512]{0:T(512)S(1)}, f32[512]{0:T(512)}, u32[]{:S(2)}) copy-start(f32[512]{0:T(512)} %param.19) | copy-start | bytes 6148
  3.6 15.8 %all-to-all-start = ((bf16[16,192,128]{2,1,0:T(8,128)(2,1)}), bf16[16,192,128]{2,1,0:T(8,128)(2,1)S(1)}, u32[]{:S(2)}, u32[]{:S(2)}) async-start(bf16[16,192,128]{2,1,0:T(8,128)(2,1)} %project.1), calls=%async_computation | async-start | bytes 1572864 | tf_op jit(solution)/shard_map/all_to_all | solution.py:252
  14.9 19.2 %copy-start = (bf16[512,1536]{1,0:T(8,128)(2,1)S(1)}, bf16[512,1536]{1,0:T(8,128)(2,1)}, u32[]{:S(2)}) copy-start(bf16[512,1536]{1,0:T(8,128)(2,1)} %proj_ref.3) | copy-start | bytes 4718596
  74.2 27.0 %copy-start.1 = (f32[512,512]{1,0:T(8,128)S(1)}, f32[512,512]{1,0:T(8,128)}, u32[]{:S(2)}) copy-start(f32[512,512]{1,0:T(8,128)} %moment_ref.1) | copy-start | bytes 3145732
  74.3 27.0 %copy-start.2 = (bf16[512,512]{1,0:T(8,128)(2,1)S(1)}, bf16[512,512]{1,0:T(8,128)(2,1)}, u32[]{:S(2)}) copy-start(bf16[512,512]{1,0:T(8,128)(2,1)} %table_ref.1) | copy-start | bytes 1572868

commit v8 on v7

--- a/solution.py
+++ b/solution.py
@@ -43,18 +43,17 @@
     rows = x_ref.shape[0]
     half = rows // 2
     count = send_ref.shape[0]
-    x = x_ref[...]
+    thirds = [
+        jnp.dot(
+            x_ref[...], proj_ref[:, third * features : third * features + features],
+            preferred_element_type=f32,
+        )
+        for third in range(3)
+    ]
     for pair in range(HEADS // 2):
         at = pair * LANES
-        parts = [
-            jnp.dot(
-                x, proj_ref[:, third * features + at : third * features + at + LANES],
-                preferred_element_type=f32,
-            )
-            for third in range(3)
-        ]
+        queries, keys, values = [third[:, at : at + LANES] for third in thirds]
         cot = grad_ref[:, at : at + LANES].astype(f32)
-        queries, keys, values = parts
         for odd, join in ((0, pair_low), (1, pair_high)):
             query_grad = join(queries, cot).astype(bf16)
             key_value = join(keys, values).astype(bf16)

time: 130 us -> 130 us (level)
  no operation moved by 1% of the time
where the time goes in v8:
time: 130 us; the launch traced here: 129 us
  blocking collectives  102 us (78%)
  Pallas kernels  10.8 us (8%)
  starting transfers between devices  9.75 us (8%)
  waiting for transfers between devices  4.19 us (3%)
  local copies, waits for them, and re-layouts  1.51 us (1%)
    all_to_all x5, blocking collectives, exchange(): lax.all_to_all(array, axis, split_axis=0, concat_axis=0, axis_index_group...  102 us
    all_to_all x1, starting transfers between devices, exchange(): lax.all_to_all(array, axis, split_axis=0, concat_axis=0, axis_index_group...  9.75 us
    all_to_all x1, waiting for transfers between devices, exchange(): lax.all_to_all(array, axis, split_axis=0, concat_axis=0, axis_index_group...  4.19 us
    pallas_call x1, Pallas kernels, body(): pl.pallas_call(functools.partial(attention_kernel, seq_shift), out_shape=...  3.53 us
    pallas_call x1, Pallas kernels, body(): pl.pallas_call(functools.partial(project_kernel, seq_shift), out_shape=sh...  2.81 us
  transfers between devices with their start and end apart: 1, of which 1 were waited for; matrix products, arithmetic and copies ran while one was open for 1% of the time, Pallas kernels for 0%

profile of v8, /device:TPU:1, one launch (start us, length us, event | category | flops | bytes accessed | tf_op | source)
XLA Modules:
  0.0 129.3 jit_solution(1007741143324151655)
XLA Ops:
  0.7 2.8 %project.1 = bf16[16,192,128]{2,1,0:T(8,128)(2,1)} custom-call(bf16[128,512]{1,0:T(8,128)(2,1)} %bitcast.42, bf16[512,1536]{1,0:T(8,128)(2,1)} %proj_ref.3, bf16[128,512]{1,0:T(8,128)(2,1)} %bitcast.43), custom_call_target="tpu_custom_call" | custom-call | tf_op jit(solution)/shard_map/project/pallas_call | solution.py:269
  3.5 9.8 %all-to-all-start = ((bf16[16,192,128]{2,1,0:T(8,128)(2,1)}), bf16[16,192,128]{2,1,0:T(8,128)(2,1)S(1)}, u32[]{:S(2)}, u32[]{:S(2)}) async-start(bf16[16,192,128]{2,1,0:T(8,128)(2,1)} %project.1), calls=%async_computation | async-start | bytes 1572864 | tf_op jit(solution)/shard_map/all_to_all | solution.py:251
  13.3 0.1 copy.16
  13.4 1.1 gather_fusion
  14.6 0.1 broadcast_in_dim.26
  14.7 0.0 copy-start
  14.8 0.1 convert_reduce_fusion
  14.9 0.1 select_convert_fusion.digits_ref
  15.0 4.2 %all-to-all-done.got_ref = bf16[16,192,128]{2,1,0:T(8,128)(2,1)S(1)} async-done(((bf16[16,192,128]{2,1,0:T(8,128)(2,1)}), bf16[16,192,128]{2,1,0:T(8,128)(2,1)S(1)}, u32[]{:S(2)}, u32[]{:S(2)}) %all-to-all-start) | async-done | bytes 786464 | tf_op jit(solution)/shard_map/all_to_all | solution.py:251
  19.2 0.0 copy-done.6
  19.2 0.1 broadcast_in_dim.30.second_ref
  19.4 3.5 %attention.1 = bf16[16,128,128]{2,1,0:T(8,128)(2,1)S(1)} custom-call(s32[1]{0:T(128)} %bitcast.part_ref, f32[16,2048]{1,0:T(8,128)S(1)} %bitcast.39, bf16[16,192,128]{2,1,0:T(8,128)(2,1)S(1)} %all-to-all-done.got_ref), custom_call_target="tpu_custom_call" | custom-call | tf_op jit(solution)/shard_map/attention/pallas_call | solution.py:304
  22.9 11.0 %all_to_all.30.got_ref = bf16[16,128,128]{2,1,0:T(8,128)(2,1)S(1)} all-to-all(bf16[16,128,128]{2,1,0:T(8,128)(2,1)S(1)} %attention.1), channel_id=1, replica_groups={{320,352,384,416,448,480,0,32,64,96,128,160,192,224,256,288},{321,353,3..., dimensions={0} | all-to-all | bytes 1048576 | tf_op jit(solution)/shard_map/all_to_all | solution.py:251
  33.9 1.0 input_grad.1
  34.9 38.4 %all_to_all.31.got_ref = bf16[32,17,2,128]{3,2,1,0:T(2,128)(2,1)S(1)} all-to-all(bf16[32,17,2,128]{3,2,1,0:T(2,128)(2,1)S(1)} %input_grad.1), channel_id=1, replica_groups={{19,20,21,22,23,24,25,26,27,28,29,30,31,0,1,2,3,4,5,6,7,8,9,10,11,12,13..., dimensions={0} | all-to-all | bytes 557056 | tf_op jit(solution)/shard_map/all_to_all | solution.py:251
  73.3 0.8 slab.1
  74.1 0.0 copy-start.1
  74.1 0.0 copy-start.2
  74.1 13.4 %all_to_all.32.got_ref = bf16[16,32,512]{2,1,0:T(8,128)(2,1)S(1)} all-to-all(bf16[16,32,512]{2,1,0:T(8,128)(2,1)S(1)} %bitcast.38), channel_id=1, replica_groups={{320,352,384,416,448,480,0,32,64,96,128,160,192,224,256,288},{321,353,3..., dimensions={0} | all-to-all | bytes 1048576 | tf_op jit(solution)/shard_map/all_to_all | solution.py:251
  87.5 0.1 row_sum.1
  87.6 13.4 %all_to_all.33 = bf16[16,32,512]{2,1,0:T(8,128)(2,1)S(1)} all-to-all(bf16[16,32,512]{2,1,0:T(8,128)(2,1)S(1)} %row_sum.1), channel_id=1, replica_groups={{320,352,384,416,448,480,0,32,64,96,128,160,192,224,256,288},{321,353,3..., dimensions={0} | all-to-all | bytes 1048576 | tf_op jit(solution)/shard_map/all_to_all | solution.py:251
  101.1 1.8 %adam.1 = (bf16[512,512]{1,0:T(8,128)(2,1)}, f32[512,512]{1,0:T(8,128)}, f32[1,512]{1,0:T(1,128)}, bf16[256,512]{1,0:T(8,128)(2,1)S(1)}) custom-call(bf16[512,512]{1,0:T(8,128)(2,1)S(1)} %bitcast.36, f32[512,512]{1,0:T(8,128)S(1)} %copy-done.1, f32[512,128]{1,0:T(8,128)S(1)} %broadcast_in_dim.30.second_ref, bf16[512,512]{1,0:T(8,128)(2,1)S(1)} %copy-done.2, ...), custom_call_target="tpu_custom_call" | custom-call | tf_op jit(solution)/shard_map/adam/pallas_call | solution.py:343
  102.8 25.5 %all_to_all.34 = bf16[32,8,512]{2,1,0:T(8,128)(2,1)S(1)} all-to-all(bf16[32,8,512]{2,1,0:T(8,128)(2,1)S(1)} %bitcast.40), channel_id=1, replica_groups={{19,20,21,22,23,24,25,26,27,28,29,30,31,0,1,2,3,4,5,6,7,8,9,10,11,12,13..., dimensions={0} | all-to-all | bytes 524288 | tf_op jit(solution)/shard_map/all_to_all | solution.py:251
  128.4 0.9 event_rows.1
  (22 shorter events, 0.2 us)
Async XLA Ops:
  0.6 12.6 %copy-start.7 = (s32[1,128]{1,0:T(1,128)S(1)}, s32[1,128]{1,0:T(1,128)}, u32[]{:S(2)}) copy-start(s32[1,128]{1,0:T(1,128)} %param.14) | copy-start | bytes 1540
  0.6 12.6 %copy-start.5 = (s32[16,16]{1,0:T(8,128)S(1)}, s32[16,16]{1,0:T(8,128)}, u32[]{:S(2)}) copy-start(s32[16,16]{1,0:T(8,128)} %param.13) | copy-start | bytes 3076
  0.7 12.7 %copy-start.3 = (s32[16384]{0:T(1024)S(1)}, s32[16384]{0:T(1024)}, u32[]{:S(2)}) copy-start(s32[16384]{0:T(1024)} %param.16) | copy-start | bytes 196612
  0.7 12.7 %copy-start.4 = (s32[16384]{0:T(1024)S(1)}, s32[16384]{0:T(1024)}, u32[]{:S(2)}) copy-start(s32[16384]{0:T(1024)} %param.15) | copy-start | bytes 196612
  3.5 15.8 %copy-start.6 = (f32[512]{0:T(512)S(1)}, f32[512]{0:T(512)}, u32[]{:S(2)}) copy-start(f32[512]{0:T(512)} %param.19) | copy-start | bytes 6148
  3.5 15.7 %all-to-all-start = ((bf16[16,192,128]{2,1,0:T(8,128)(2,1)}), bf16[16,192,128]{2,1,0:T(8,128)(2,1)S(1)}, u32[]{:S(2)}, u32[]{:S(2)}) async-start(bf16[16,192,128]{2,1,0:T(8,128)(2,1)} %project.1), calls=%async_computation | async-start | bytes 1572864 | tf_op jit(solution)/shard_map/all_to_all | solution.py:251
  14.7 19.2 %copy-start = (bf16[512,1536]{1,0:T(8,128)(2,1)S(1)}, bf16[512,1536]{1,0:T(8,128)(2,1)}, u32[]{:S(2)}) copy-start(bf16[512,1536]{1,0:T(8,128)(2,1)} %proj_ref.3) | copy-start | bytes 4718596
  74.1 27.0 %copy-start.1 = (f32[512,512]{1,0:T(8,128)S(1)}, f32[512,512]{1,0:T(8,128)}, u32[]{:S(2)}) copy-start(f32[512,512]{1,0:T(8,128)} %moment_ref.1) | copy-start | bytes 3145732
  74.1 27.0 %copy-start.2 = (bf16[512,512]{1,0:T(8,128)(2,1)S(1)}, bf16[512,512]{1,0:T(8,128)(2,1)}, u32[]{:S(2)}) copy-start(bf16[512,512]{1,0:T(8,128)(2,1)} %table_ref.1) | copy-start | bytes 1572868
